TPU v7x, 32 devices: a whole 2x2x4 slice. The times are simulated.
32 devices in a mesh: gz: 2 (over x), ax: 4 (over y, core), ay: 4 (over z).
Axes of the slice: x: 2, y: 2, z: 4, core: 2. Of those that a mesh axis runs over, the one named last changes fastest.
Arguments:
- source: float32 [64, 256, 512], P('gz', 'ax', 'ay'), may hold values from -120 to 120
- pressure: float32 [64, 256, 512], P('gz', 'ax', 'ay'), may hold values from -0.12 to 0.12
- storage: float32 [64, 256, 512], P('gz', 'ax', 'ay'), may hold values from 0.1 to 1
- trans_z: float32 [64, 256, 512], P('gz', 'ax', 'ay'), may hold values from 100 to 10000
- trans_x: float32 [64, 256, 512], P('gz', 'ax', 'ay'), may hold values from 0.3 to 3
- trans_y: float32 [64, 256, 512], P('gz', 'ax', 'ay'), may hold values from 0.3 to 3
Outputs:
- smoothed: float32 [64, 256, 512], P('gz', 'ax', 'ay')
- residual: float32 [64, 256, 512], P('gz', 'ax', 'ay')
All inputs are finite; a program needn't handle non-finite values.
Results may differ from a plain program's by a relative error of at most 0.00035.
Values sent between devices are 32-bit elements; how exact they have to be, the bound alone decides.
No kernel may reach another device: no remote copies, remote signals or barrier semaphores. Data moves between devices by JAX's collectives and lax.ppermute only.
A program may use at most 128 MiB of HBM per device.

v0:
```python
import jax
import jax.numpy as jnp
from jax import lax
from jax.sharding import PartitionSpec as P

SWEEPS = 2


OMEGA = 0.8


def with_halo(cells, sides, width):
    for axis, dim in sides:
        count = lax.axis_size(axis)
        ends = count - 1
        head = lax.slice_in_dim(cells, 0, width, axis=dim)
        tail = lax.slice_in_dim(cells, cells.shape[dim] - width, cells.shape[dim], axis=dim)
        cells = jnp.concatenate(
            [
                lax.ppermute(tail, axis, [(i, (i + 1) % count) for i in range(ends)]),
                cells,
                lax.ppermute(head, axis, [((i + 1) % count, i) for i in range(ends)]),
            ],
            axis=dim,
        )
    return cells


def shifted(value, axis, steps):
    count = lax.axis_size(axis)
    leading, last = (max(0, -steps), min(count, count - steps))
    return lax.ppermute(value, axis, [(source, source + steps) for source in range(leading, last)])


def band_solve(diag, upper, lower, rhs):
    d_line = jnp.moveaxis(diag, 0, -1)
    du_line = jnp.moveaxis(upper, 0, -1)
    dl_line = jnp.moveaxis(lower, 0, -1)
    b_line = jnp.moveaxis(rhs, 0, -2)
    solution = lax.linalg.tridiagonal_solve(dl_line, d_line, du_line, b_line)
    return jnp.moveaxis(solution, -2, 0)


def edge_mask(field, axis, count, position):
    local = lax.broadcasted_iota(jnp.int32, field.shape, axis)
    width = field.shape[axis]
    total = width * count
    return (position * width + local < total - 1).astype(jnp.float32)


def areal_side(field, source, cx, cx_w, cy, cy_w):
    padded = with_halo(field, (("ax", 1), ("ay", 2)), 1)
    line = source + cx * padded[:, 2:, 1:-1] + cx_w * padded[:, :-2, 1:-1]
    return line + cy * padded[:, 1:-1, 2:] + cy_w * padded[:, 1:-1, :-2]


def body(source, pressure, storage, trans_z, trans_x, trans_y):
    cz = trans_z * edge_mask(trans_z, 0, lax.axis_size("gz"), lax.axis_index("gz"))
    cx = trans_x * edge_mask(trans_x, 1, lax.axis_size("ax"), lax.axis_index("ax"))
    cy = trans_y * edge_mask(trans_y, 2, lax.axis_size("ay"), lax.axis_index("ay"))
    below_face = shifted(cz[-1:], "gz", 1)
    west_face = shifted(cx[:, -1:], "ax", 1)
    south_face = shifted(cy[:, :, -1:], "ay", 1)
    cz_b = jnp.concatenate([below_face, cz[:-1]], 0)
    cx_w = jnp.concatenate([west_face, cx[:, :-1]], 1)
    cy_w = jnp.concatenate([south_face, cy[:, :, :-1]], 2)
    diag = storage + cz + cz_b + cx + cx_w + cy + cy_w
    field = pressure
    lower = -cz_b
    upper = -cz
    depth = diag.shape[0]
    inner_diag = diag[1:-1]
    inner_upper = upper[1:-1]
    inner_lower = lower[1:-1]
    blank = jnp.zeros_like(diag[: depth - 3])
    first_term = jnp.concatenate([lower[1:2], blank], 0)
    last_term = jnp.concatenate([blank, upper[depth - 2 : depth - 1]], 0)
    spikes = band_solve(
        inner_diag, inner_upper, inner_lower, jnp.stack([first_term, last_term], -1)
    )
    left_spike = spikes[..., 0]
    right_spike = spikes[..., 1]
    sub_pair = jnp.stack([lower[0], -lower[-1] * left_spike[-1]], 0)
    mid_pair = jnp.stack(
        [diag[0] - upper[0] * left_spike[0], diag[-1] - lower[-1] * right_spike[-1]], 0
    )
    sup_pair = jnp.stack([-upper[0] * right_spike[0], upper[-1]], 0)
    sub_all, mid_all, sup_all = (
        lax.all_gather(sub_pair, "gz", axis=0, tiled=True),
        lax.all_gather(mid_pair, "gz", axis=0, tiled=True),
        lax.all_gather(sup_pair, "gz", axis=0, tiled=True),
    )
    block = lax.axis_index("gz")
    for sweep in range(SWEEPS):
        line = areal_side(field, source, cx, cx_w, cy, cy_w)
        inner = band_solve(inner_diag, inner_upper, inner_lower, line[1:-1, :, :, None])[..., 0]
        side_pair = jnp.stack([line[0] - upper[0] * inner[0], line[-1] - lower[-1] * inner[-1]], 0)
        sides = lax.all_gather(side_pair, "gz", axis=0, tiled=True)
        reduced = band_solve(mid_all, sup_all, sub_all, sides[..., None])[..., 0]
        ends = lax.dynamic_slice_in_dim(reduced, 2 * block, 2, 0)
        middle = inner - left_spike * ends[0] - right_spike * ends[1]
        solution = jnp.concatenate([ends[:1], middle, ends[1:]], 0)
        field = field + OMEGA * (solution - field)
    padded = with_halo(field, (("gz", 0), ("ax", 1), ("ay", 2)), 1)
    applied = diag * field - cz * padded[2:, 1:-1, 1:-1] - cz_b * padded[:-2, 1:-1, 1:-1]
    applied = applied - cx * padded[1:-1, 2:, 1:-1] - cx_w * padded[1:-1, :-2, 1:-1]
    applied = applied - cy * padded[1:-1, 1:-1, 2:] - cy_w * padded[1:-1, 1:-1, :-2]
    return (field, source - applied)


def solution(mesh):
    return jax.shard_map(
        body,
        mesh=mesh,
        in_specs=(
            P("gz", "ax", "ay"),
            P("gz", "ax", "ay"),
            P("gz", "ax", "ay"),
            P("gz", "ax", "ay"),
            P("gz", "ax", "ay"),
            P("gz", "ax", "ay"),
        ),
        out_specs=(P("gz", "ax", "ay"), P("gz", "ax", "ay")),
        check_vma=False,
    )
```

profile of v0, /device:TPU:25, one launch (start us, length us, event | category | flops | bytes accessed | tf_op | source)
XLA Modules:
  0.0 185.6 jit_solution(12079497044481090204)
XLA Ops:
  1.6 2.6 %collective-permute-start = (f32[32,1,128]{2,0,1:T(8,128)S(1)}, f32[32,1,128]{2,0,1:T(8,128)S(1)}, u32[]{:S(2)}, u32[]{:S(2)}) collective-permute-start(f32[32,1,128]{2,0,1:T(8,128)S(1)} %bitcast.2341), channel_id=1, source_target_pairs={{4,0},{8,4},{12,8},{5,1},{9,5},{13,9},{6,2},{10,6},{14,10},{7,3},{... | collective-permute-start | bytes 49160 | tf_op jit(solution)/shard_map/ppermute | solution.py:22
  4.2 3.0 %collective-permute-start.2 = (f32[32,1,128]{2,0,1:T(8,128)S(1)}, f32[32,1,128]{2,0,1:T(8,128)S(1)}, u32[]{:S(2)}, u32[]{:S(2)}) collective-permute-start(f32[32,1,128]{2,0,1:T(8,128)S(1)} %bitcast.2340), channel_id=1, source_target_pairs={{0,4},{4,8},{8,12},{1,5},{5,9},{9,13},{2,6},{6,10},{10,14},{3,7},{... | collective-permute-start | bytes 49160 | tf_op jit(solution)/shard_map/ppermute | solution.py:20
  7.3 3.0 %copy_select_fusion = (f32[32,64,128]{2,0,1:T(8,128)S(1)}, f32[32,64,128]{2,0,1:T(8,128)S(1)}) fusion(f32[32,64,128]{2,1,0:T(8,128)} %param.11, pred[128]{0:T(512)(128)(4,1)S(1)} %add_compare_fusion.1, f32[32,64,128]{2,1,0:T(8,128)} %param.10, pred[64]{0:T(512)(128)(4,1)S(1)} %add_compare_fusion.2), kind=kLoop, calls=%fused_computation.72 | loop fusion | flops 524288 | bytes 4194496 | tf_op jit(solution)/shard_map/mul | solution.py:60
  10.3 2.4 %collective-permute-start.1 = (f32[32,1,128]{2,0,1:T(8,128)S(1)}, f32[32,1,128]{2,0,1:T(8,128)S(1)}, u32[]{:S(2)}, u32[]{:S(2)}) collective-permute-start(f32[32,1,128]{2,0,1:T(8,128)S(1)} %slice.1340), channel_id=1, source_target_pairs={{0,4},{4,8},{8,12},{1,5},{5,9},{9,13},{2,6},{6,10},{10,14},{3,7},{... | collective-permute-start | bytes 49160 | tf_op jit(solution)/shard_map/ppermute | solution.py:32
  16.5 3.1 %collective-permute-start.6 = (f32[1,64,128]{2,1,0:T(8,128)S(1)}, f32[1,64,128]{2,1,0:T(8,128)S(1)}, u32[]{:S(2)}, u32[]{:S(2)}) collective-permute-start(f32[1,64,128]{2,1,0:T(8,128)S(1)} %slice.1350), channel_id=1, source_target_pairs={{0,16},{1,17},{2,18},{3,19},{4,20},{5,21},{6,22},{7,23},{8,24},{9,... | collective-permute-start | bytes 98312 | tf_op jit(solution)/shard_map/ppermute | solution.py:32
  27.9 4.8 %collective-permute-start.3 = (f32[32,66,1]{1,0,2:T(8,128)S(1)}, f32[32,66,1]{1,0,2:T(8,128)S(1)}, u32[]{:S(2)}, u32[]{:S(2)}) collective-permute-start(f32[32,66,1]{1,0,2:T(8,128)S(1)} %copy.273), channel_id=1, source_target_pairs={{1,0},{2,1},{3,2},{5,4},{6,5},{7,6},{9,8},{10,9},{11,10},{13,12},{... | collective-permute-start | bytes 25352 | tf_op jit(solution)/shard_map/ppermute | solution.py:22
  35.9 1.8 copy.469
  43.8 6.7 %fusion.16 = (f32[32,64,128]{2,1,0:T(8,128)S(1)}, f32[32,64,128]{2,1,0:T(8,128)S(1)}) fusion(f32[32,66,1]{2,1,0:T(8,128)} %copy.280, f32[32,1,128]{2,1,0:T(1,128)S(1)} %bitcast.2333, f32[32,64,128]{2,1,0:T(8,128)} %param.7, f32[32,1,128]{2,1,0:T(1,128)S(1)} %bitcast.2335, f32[32,66,1]{2,1,0:T(8,128)} %copy.274, f32[32,64,128]{2,1,0:T(8,128)} %param.6, ...), kind=kLoop, calls=%fused_computation.43 | loop fusion | flops 4718592 | bytes 8438272 | tf_op jit(solution)/shard_map/add | solution.py:54
  68.3 3.8 %all_gather.18 = f32[4,64,128]{2,1,0:T(8,128)S(1)} all-gather(f32[2,64,128]{2,1,0:T(8,128)S(1)} %pad_maximum_fusion.38), channel_id=1, replica_groups=mesh['gz'=2,'ax'=4,'ay'=4] {'gz'}, dimensions={0}, use_global_device_ids=true | all-gather | bytes 196608 | tf_op jit(solution)/shard_map/all_gather | solution.py:89
  72.1 3.8 %all_gather.16 = f32[4,64,128]{2,1,0:T(8,128)S(1)} all-gather(f32[2,64,128]{2,1,0:T(8,128)S(1)} %pad_maximum_fusion.36), channel_id=1, replica_groups=mesh['gz'=2,'ax'=4,'ay'=4] {'gz'}, dimensions={0}, use_global_device_ids=true | all-gather | bytes 196608 | tf_op jit(solution)/shard_map/all_gather | solution.py:90
  75.9 3.8 %all_gather.17 = f32[4,64,128]{2,1,0:T(8,128)S(1)} all-gather(f32[2,64,128]{2,1,0:T(8,128)S(1)} %pad_maximum_fusion.37), channel_id=1, replica_groups=mesh['gz'=2,'ax'=4,'ay'=4] {'gz'}, dimensions={0}, use_global_device_ids=true | all-gather | bytes 196608 | tf_op jit(solution)/shard_map/all_gather | solution.py:91
  79.7 4.3 %all_gather.15 = f32[4,64,128]{2,1,0:T(8,128)S(1)} all-gather(f32[2,64,128]{2,1,0:T(8,128)S(1)} %pad_maximum_fusion.35), channel_id=1, replica_groups=mesh['gz'=2,'ax'=4,'ay'=4] {'gz'}, dimensions={0}, use_global_device_ids=true | all-gather | bytes 196608 | tf_op jit(solution)/shard_map/all_gather | solution.py:98
  86.8 7.4 %collective-permute-start.7 = (f32[32,1,128]{2,0,1:T(8,128)S(1)}, f32[32,1,128]{2,0,1:T(8,128)S(1)}, u32[]{:S(2)}, u32[]{:S(2)}) collective-permute-start(f32[32,1,128]{2,0,1:T(8,128)S(1)} %bitcast.2343), channel_id=1, source_target_pairs={{4,0},{8,4},{12,8},{5,1},{9,5},{13,9},{6,2},{10,6},{14,10},{7,3},{... | collective-permute-start | bytes 49160 | tf_op jit(solution)/shard_map/ppermute | solution.py:22
  94.2 1.9 %collective-permute-start.8 = (f32[32,1,128]{2,0,1:T(8,128)S(1)}, f32[32,1,128]{2,0,1:T(8,128)S(1)}, u32[]{:S(2)}, u32[]{:S(2)}) collective-permute-start(f32[32,1,128]{2,0,1:T(8,128)S(1)} %bitcast.2342), channel_id=1, source_target_pairs={{0,4},{4,8},{8,12},{1,5},{5,9},{9,13},{2,6},{6,10},{10,14},{3,7},{... | collective-permute-start | bytes 49160 | tf_op jit(solution)/shard_map/ppermute | solution.py:20
  99.8 2.3 %copy.380 = f32[32,66,1]{1,0,2:T(8,128)} copy(f32[32,66,1]{2,1,0:T(8,128)} %get-tuple-element.207) | data formatting | bytes 16896 | tf_op jit(solution)/shard_map/slice | solution.py:16
  102.1 4.5 %collective-permute-start.9 = (f32[32,66,1]{1,0,2:T(8,128)}, f32[32,66,1]{1,0,2:T(8,128)}, u32[]{:S(2)}, u32[]{:S(2)}) collective-permute-start(f32[32,66,1]{1,0,2:T(8,128)} %copy.380), channel_id=1, source_target_pairs={{1,0},{2,1},{3,2},{5,4},{6,5},{7,6},{9,8},{10,9},{11,10},{13,12},{... | collective-permute-start | bytes 25352 | tf_op jit(solution)/shard_map/ppermute | solution.py:22
  106.6 2.3 %copy.384 = f32[32,66,1]{1,0,2:T(8,128)} copy(f32[32,66,1]{2,1,0:T(8,128)} %get-tuple-element.208) | data formatting | bytes 16896 | tf_op jit(solution)/shard_map/slice | solution.py:17
  110.2 2.2 %copy.381 = f32[32,66,1]{2,1,0:T(8,128)} copy(f32[32,66,1]{1,0,2:T(8,128)} %collective-permute-done.9) | data formatting | bytes 16896 | tf_op jit(solution)/shard_map/ppermute | solution.py:22
  113.7 2.3 %copy.385 = f32[32,66,1]{2,1,0:T(8,128)} copy(f32[32,66,1]{1,0,2:T(8,128)} %collective-permute-done.10) | data formatting | bytes 16896 | tf_op jit(solution)/shard_map/ppermute | solution.py:20
  116.0 5.6 %pad_maximum_fusion.17 = (f32[32,64,128]{2,1,0:T(8,128)S(1)}, f32[32,64,128]{2,1,0:T(8,128)S(1)}, f32[32,64,128]{2,1,0:T(8,128)S(1)}) fusion(f32[32,66,1]{2,1,0:T(8,128)} %copy.381, f32[32,1,128]{2,1,0:T(1,128)} %bitcast.2337, f32[32,64,128]{2,1,0:T(8,128)} %copy-done, f32[32,1,128]{2,1,0:T(1,128)} %bitcast.2339, f32[32,63,128]{2,1,0:T(8,128)S(1)} %copy.469, ...), kind=kLoop, calls=%fused_computation.32 | loop fusion | flops 3670016 | bytes 8438272 | tf_op jit(solution)/shard_map/concatenate | solution.py:18
  129.2 3.8 %all_gather.19 = f32[4,64,128]{2,1,0:T(8,128)S(1)} all-gather(f32[2,64,128]{2,1,0:T(8,128)S(1)} %copy.390), channel_id=1, replica_groups=mesh['gz'=2,'ax'=4,'ay'=4] {'gz'}, dimensions={0}, use_global_device_ids=true | all-gather | bytes 196608 | tf_op jit(solution)/shard_map/all_gather | solution.py:98
  136.2 1.9 %collective-permute-start.12 = (f32[1,64,128]{2,1,0:T(8,128)S(1)}, f32[1,64,128]{2,1,0:T(8,128)S(1)}, u32[]{:S(2)}, u32[]{:S(2)}) collective-permute-start(f32[1,64,128]{2,1,0:T(8,128)S(1)} %get-tuple-element.223), channel_id=1, source_target_pairs={{0,16},{1,17},{2,18},{3,19},{4,20},{5,21},{6,22},{7,23},{8,24},{9,... | collective-permute-start | bytes 98312 | tf_op jit(solution)/shard_map/ppermute | solution.py:20
  139.4 3.3 %collective-permute-done.11 = f32[1,64,128]{2,1,0:T(8,128)S(1)} collective-permute-done((f32[1,64,128]{2,1,0:T(8,128)S(1)}, f32[1,64,128]{2,1,0:T(8,128)S(1)}, u32[]{:S(2)}, u32[]{:S(2)}) %collective-permute-start.11) | collective-permute-done | bytes 32800 | tf_op jit(solution)/shard_map/ppermute | solution.py:22
  142.9 7.6 %collective-permute-start.14 = (f32[34,1,128]{2,1,0:T(1,128)S(1)}, f32[34,1,128]{2,1,0:T(1,128)S(1)}, u32[]{:S(2)}, u32[]{:S(2)}) collective-permute-start(f32[34,1,128]{2,1,0:T(1,128)S(1)} %get-tuple-element.215), channel_id=1, source_target_pairs={{0,4},{4,8},{8,12},{1,5},{5,9},{9,13},{2,6},{6,10},{10,14},{3,7},{... | collective-permute-start | bytes 52232 | tf_op jit(solution)/shard_map/ppermute | solution.py:20
  150.5 1.9 %collective-permute-start.13 = (f32[34,1,128]{2,1,0:T(1,128)S(1)}, f32[34,1,128]{2,1,0:T(1,128)S(1)}, u32[]{:S(2)}, u32[]{:S(2)}) collective-permute-start(f32[34,1,128]{2,1,0:T(1,128)S(1)} %get-tuple-element.214), channel_id=1, source_target_pairs={{4,0},{8,4},{12,8},{5,1},{9,5},{13,9},{6,2},{10,6},{14,10},{7,3},{... | collective-permute-start | bytes 52232 | tf_op jit(solution)/shard_map/ppermute | solution.py:22
  153.1 2.4 %collective-permute-done.13 = f32[34,1,128]{2,1,0:T(1,128)S(1)} collective-permute-done((f32[34,1,128]{2,1,0:T(1,128)S(1)}, f32[34,1,128]{2,1,0:T(1,128)S(1)}, u32[]{:S(2)}, u32[]{:S(2)}) %collective-permute-start.13) | collective-permute-done | bytes 17440 | tf_op jit(solution)/shard_map/ppermute | solution.py:22
  155.6 2.0 %fusion.448 = (f32[34,66,1]{2,0,1:T(8,128)}, f32[34,66,1]{2,0,1:T(8,128)}) fusion(f32[34,66,128]{2,0,1:T(8,128)S(1)} %constant_dynamic-update-slice_fusion.87), kind=kLoop, calls=%fused_computation.907 | loop fusion | bytes 35904 | tf_op jit(solution)/shard_map/slice | solution.py:16
  157.6 1.9 %copy.397 = f32[34,66,1]{1,0,2:T(8,128)S(1)} copy(f32[34,66,1]{2,0,1:T(8,128)} %get-tuple-element.205) | data formatting | bytes 17952 | tf_op jit(solution)/shard_map/slice | solution.py:16
  159.5 1.9 %copy.399 = f32[34,66,1]{1,0,2:T(8,128)S(1)} copy(f32[34,66,1]{2,0,1:T(8,128)} %get-tuple-element.206) | data formatting | bytes 17952 | tf_op jit(solution)/shard_map/slice | solution.py:17
  162.6 4.2 %collective-permute-start.15 = (f32[34,66,1]{1,0,2:T(8,128)S(1)}, f32[34,66,1]{1,0,2:T(8,128)S(1)}, u32[]{:S(2)}, u32[]{:S(2)}) collective-permute-start(f32[34,66,1]{1,0,2:T(8,128)S(1)} %copy.397), channel_id=1, source_target_pairs={{1,0},{2,1},{3,2},{5,4},{6,5},{7,6},{9,8},{10,9},{11,10},{13,12},{... | collective-permute-start | bytes 26936 | tf_op jit(solution)/shard_map/ppermute | solution.py:22
  166.9 6.3 %pad_maximum_fusion.9 = (f32[32,64,128]{2,1,0:T(8,128)}, f32[32,64,128]{2,1,0:T(8,128)}, f32[32,64,128]{2,1,0:T(8,128)}) fusion(f32[34,1,128]{2,1,0:T(1,128)S(1)} %collective-permute-done.13, f32[1,64,128]{2,1,0:T(8,128)S(1)} %collective-permute-done.11, f32[32,64,128]{2,1,0:T(8,128)} %copy-done.9, f32[1,64,128]{2,1,0:T(8,128)S(1)} %collective-permute-done.12, ...), kind=kLoop, calls=%fused_computation.19 | loop fusion | flops 4194304 | bytes 8488960 | tf_op jit(solution)/shard_map/concatenate | solution.py:18
  176.6 7.4 %fusion.2 = f32[32,64,128]{2,0,1:T(8,128)S(1)} fusion(f32[34,66,128]{2,0,1:T(8,128)} %copy-done.8, f32[34,66,1]{2,0,1:T(8,128)} %copy.400, f32[32,64,128]{2,0,1:T(8,128)S(1)} %get-tuple-element.273, f32[34,66,1]{2,0,1:T(8,128)} %copy.398, f32[32,64,128]{2,1,0:T(8,128)} %param.6, f32[32,64,128]{2,1,0:T(8,128)S(1)} %copy-done.5, ...), kind=kLoop, calls=%fused_computation.11 | loop fusion | flops 2621440 | bytes 9555488 | tf_op jit(solution)/shard_map/sub | solution.py:108
  (422 shorter events, 65.9 us)
Async XLA Ops:
  1.6 19.1 %collective-permute-start = (f32[32,1,128]{2,0,1:T(8,128)S(1)}, f32[32,1,128]{2,0,1:T(8,128)S(1)}, u32[]{:S(2)}, u32[]{:S(2)}) collective-permute-start(f32[32,1,128]{2,0,1:T(8,128)S(1)} %bitcast.2341), channel_id=1, source_target_pairs={{4,0},{8,4},{12,8},{5,1},{9,5},{13,9},{6,2},{10,6},{14,10},{7,3},{... | collective-permute-start | bytes 49160 | tf_op jit(solution)/shard_map/ppermute | solution.py:22
  4.2 16.6 %collective-permute-start.2 = (f32[32,1,128]{2,0,1:T(8,128)S(1)}, f32[32,1,128]{2,0,1:T(8,128)S(1)}, u32[]{:S(2)}, u32[]{:S(2)}) collective-permute-start(f32[32,1,128]{2,0,1:T(8,128)S(1)} %bitcast.2340), channel_id=1, source_target_pairs={{0,4},{4,8},{8,12},{1,5},{5,9},{9,13},{2,6},{6,10},{10,14},{3,7},{... | collective-permute-start | bytes 49160 | tf_op jit(solution)/shard_map/ppermute | solution.py:20
  10.3 33.4 %collective-permute-start.1 = (f32[32,1,128]{2,0,1:T(8,128)S(1)}, f32[32,1,128]{2,0,1:T(8,128)S(1)}, u32[]{:S(2)}, u32[]{:S(2)}) collective-permute-start(f32[32,1,128]{2,0,1:T(8,128)S(1)} %slice.1340), channel_id=1, source_target_pairs={{0,4},{4,8},{8,12},{1,5},{5,9},{9,13},{2,6},{6,10},{10,14},{3,7},{... | collective-permute-start | bytes 49160 | tf_op jit(solution)/shard_map/ppermute | solution.py:32
  13.7 25.6 %collective-permute-start.4 = (f32[32,64,1]{1,0,2:T(8,128)S(1)}, f32[32,64,1]{1,0,2:T(8,128)S(1)}, u32[]{:S(2)}, u32[]{:S(2)}) collective-permute-start(f32[32,64,1]{1,0,2:T(8,128)S(1)} %copy.276), channel_id=1, source_target_pairs={{0,1},{1,2},{2,3},{4,5},{5,6},{6,7},{8,9},{9,10},{10,11},{12,13},{... | collective-permute-start | bytes 24584 | tf_op jit(solution)/shard_map/ppermute | solution.py:32
  16.4 18.4 %copy-start.2 = (f32[32,64,128]{2,1,0:T(8,128)}, f32[32,64,128]{2,1,0:T(8,128)S(1)}, u32[]{:S(2)}) copy-start(f32[32,64,128]{2,1,0:T(8,128)S(1)} %get-tuple-element.198) | copy-start | bytes 3145732
  16.5 34.2 %collective-permute-start.6 = (f32[1,64,128]{2,1,0:T(8,128)S(1)}, f32[1,64,128]{2,1,0:T(8,128)S(1)}, u32[]{:S(2)}, u32[]{:S(2)}) collective-permute-start(f32[1,64,128]{2,1,0:T(8,128)S(1)} %slice.1350), channel_id=1, source_target_pairs={{0,16},{1,17},{2,18},{3,19},{4,20},{5,21},{6,22},{7,23},{8,24},{9,... | collective-permute-start | bytes 98312 | tf_op jit(solution)/shard_map/ppermute | solution.py:32
  26.6 15.6 %collective-permute-start.5 = (f32[32,66,1]{1,0,2:T(8,128)S(1)}, f32[32,66,1]{1,0,2:T(8,128)S(1)}, u32[]{:S(2)}, u32[]{:S(2)}) collective-permute-start(f32[32,66,1]{1,0,2:T(8,128)S(1)} %copy.279), channel_id=1, source_target_pairs={{0,1},{1,2},{2,3},{4,5},{5,6},{6,7},{8,9},{9,10},{10,11},{12,13},{... | collective-permute-start | bytes 25352 | tf_op jit(solution)/shard_map/ppermute | solution.py:20
  27.9 12.8 %collective-permute-start.3 = (f32[32,66,1]{1,0,2:T(8,128)S(1)}, f32[32,66,1]{1,0,2:T(8,128)S(1)}, u32[]{:S(2)}, u32[]{:S(2)}) collective-permute-start(f32[32,66,1]{1,0,2:T(8,128)S(1)} %copy.273), channel_id=1, source_target_pairs={{1,0},{2,1},{3,2},{5,4},{6,5},{7,6},{9,8},{10,9},{11,10},{13,12},{... | collective-permute-start | bytes 25352 | tf_op jit(solution)/shard_map/ppermute | solution.py:22
  54.4 12.4 %copy-start.12 = (f32[32,64,128]{2,1,0:T(8,128)}, f32[32,64,128]{2,1,0:T(8,128)S(1)}, u32[]{:S(2)}) copy-start(f32[32,64,128]{2,1,0:T(8,128)S(1)} %get-tuple-element.230) | copy-start | bytes 3145732
  54.4 12.4 %copy-start.19 = (f32[32,64,128]{2,1,0:T(8,128)}, f32[32,64,128]{2,1,0:T(8,128)S(1)}, u32[]{:S(2)}) copy-start(f32[32,64,128]{2,1,0:T(8,128)S(1)} %get-tuple-element.231) | copy-start | bytes 3145732
  58.8 6.7 %copy-start.32 = (f32[64,128,1]{1,0,2:T(8,128)}, f32[64,128,1]{1,0,2:T(8,128)S(1)}, u32[]{:S(2)}) copy-start(f32[64,128,1]{1,0,2:T(8,128)S(1)} %get-tuple-element.128) | copy-start | bytes 98308
  58.8 6.8 %copy-start.30 = (f32[64,128,1]{1,0,2:T(8,128)}, f32[64,128,1]{1,0,2:T(8,128)S(1)}, u32[]{:S(2)}) copy-start(f32[64,128,1]{1,0,2:T(8,128)S(1)} %get-tuple-element.124) | copy-start | bytes 98308
  58.8 6.8 %copy-start.28 = (f32[64,128,1]{1,0,2:T(8,128)}, f32[64,128,1]{1,0,2:T(8,128)S(1)}, u32[]{:S(2)}) copy-start(f32[64,128,1]{1,0,2:T(8,128)S(1)} %get-tuple-element.120) | copy-start | bytes 98308
  58.8 6.8 %copy-start.26 = (f32[64,128,1]{1,0,2:T(8,128)}, f32[64,128,1]{1,0,2:T(8,128)S(1)}, u32[]{:S(2)}) copy-start(f32[64,128,1]{1,0,2:T(8,128)S(1)} %get-tuple-element.116) | copy-start | bytes 98308
  66.3 19.0 %copy-start.16 = (f32[30,64,128,2]{2,1,0,3:T(8,128)}, f32[30,64,128,2]{2,1,0,3:T(8,128)S(1)}, u32[]{:S(2)}) copy-start(f32[30,64,128,2]{2,1,0,3:T(8,128)S(1)} %get-tuple-element.203) | copy-start | bytes 5898244
  66.5 18.8 %copy-start.14 = (f32[64,128,30,2]{1,0,3,2:T(8,128)}, f32[64,128,30,2]{1,0,3,2:T(8,128)S(1)}, u32[]{:S(2)}) copy-start(f32[64,128,30,2]{1,0,3,2:T(8,128)S(1)} %copy.470) | copy-start | bytes 5898244
  72.1 12.7 %copy-start.55 = (f32[3,64,128]{2,1,0:T(8,128)}, f32[3,64,128]{2,1,0:T(8,128)S(1)}, u32[]{:S(2)}) copy-start(f32[3,64,128]{2,1,0:T(8,128)S(1)} %slice_bitcast_fusion.15) | copy-start | bytes 294916
  75.9 8.9 %copy-start.53 = (f32[4,64,128]{2,1,0:T(8,128)}, f32[4,64,128]{2,1,0:T(8,128)S(1)}, u32[]{:S(2)}) copy-start(f32[4,64,128]{2,1,0:T(8,128)S(1)} %all_gather.16) | copy-start | bytes 393220
  86.8 10.5 %copy-start = (f32[32,64,128]{2,1,0:T(8,128)}, f32[32,64,128]{2,1,0:T(8,128)S(1)}, u32[]{:S(2)}) copy-start(f32[32,64,128]{2,1,0:T(8,128)S(1)} %fusion.24) | copy-start | bytes 3145732
  86.8 9.3 %collective-permute-start.7 = (f32[32,1,128]{2,0,1:T(8,128)S(1)}, f32[32,1,128]{2,0,1:T(8,128)S(1)}, u32[]{:S(2)}, u32[]{:S(2)}) collective-permute-start(f32[32,1,128]{2,0,1:T(8,128)S(1)} %bitcast.2343), channel_id=1, source_target_pairs={{4,0},{8,4},{12,8},{5,1},{9,5},{13,9},{6,2},{10,6},{14,10},{7,3},{... | collective-permute-start | bytes 49160 | tf_op jit(solution)/shard_map/ppermute | solution.py:22
  94.2 3.1 %collective-permute-start.8 = (f32[32,1,128]{2,0,1:T(8,128)S(1)}, f32[32,1,128]{2,0,1:T(8,128)S(1)}, u32[]{:S(2)}, u32[]{:S(2)}) collective-permute-start(f32[32,1,128]{2,0,1:T(8,128)S(1)} %bitcast.2342), channel_id=1, source_target_pairs={{0,4},{4,8},{8,12},{1,5},{5,9},{9,13},{2,6},{6,10},{10,14},{3,7},{... | collective-permute-start | bytes 49160 | tf_op jit(solution)/shard_map/ppermute | solution.py:20
  102.1 8.1 %collective-permute-start.9 = (f32[32,66,1]{1,0,2:T(8,128)}, f32[32,66,1]{1,0,2:T(8,128)}, u32[]{:S(2)}, u32[]{:S(2)}) collective-permute-start(f32[32,66,1]{1,0,2:T(8,128)} %copy.380), channel_id=1, source_target_pairs={{1,0},{2,1},{3,2},{5,4},{6,5},{7,6},{9,8},{10,9},{11,10},{13,12},{... | collective-permute-start | bytes 25352 | tf_op jit(solution)/shard_map/ppermute | solution.py:22
  108.9 4.8 %collective-permute-start.10 = (f32[32,66,1]{1,0,2:T(8,128)}, f32[32,66,1]{1,0,2:T(8,128)}, u32[]{:S(2)}, u32[]{:S(2)}) collective-permute-start(f32[32,66,1]{1,0,2:T(8,128)} %copy.384), channel_id=1, source_target_pairs={{0,1},{1,2},{2,3},{4,5},{5,6},{6,7},{8,9},{9,10},{10,11},{12,13},{... | collective-permute-start | bytes 25352 | tf_op jit(solution)/shard_map/ppermute | solution.py:20
  128.0 6.7 %copy-start.15 = (f32[64,128,30,2]{1,0,3,2:T(8,128)S(1)}, f32[64,128,30,2]{1,0,3,2:T(8,128)}, u32[]{:S(2)}) copy-start(f32[64,128,30,2]{1,0,3,2:T(8,128)} %copy-done.14) | copy-start | bytes 5898244
  136.2 17.0 %copy-start.9 = (f32[32,64,128]{2,1,0:T(8,128)}, f32[32,64,128]{2,1,0:T(8,128)S(1)}, u32[]{:S(2)}) copy-start(f32[32,64,128]{2,1,0:T(8,128)S(1)} %fusion.26) | copy-start | bytes 3145732
  136.2 3.2 %collective-permute-start.12 = (f32[1,64,128]{2,1,0:T(8,128)S(1)}, f32[1,64,128]{2,1,0:T(8,128)S(1)}, u32[]{:S(2)}, u32[]{:S(2)}) collective-permute-start(f32[1,64,128]{2,1,0:T(8,128)S(1)} %get-tuple-element.223), channel_id=1, source_target_pairs={{0,16},{1,17},{2,18},{3,19},{4,20},{5,21},{6,22},{7,23},{8,24},{9,... | collective-permute-start | bytes 98312 | tf_op jit(solution)/shard_map/ppermute | solution.py:20
  138.1 4.7 %collective-permute-start.11 = (f32[1,64,128]{2,1,0:T(8,128)S(1)}, f32[1,64,128]{2,1,0:T(8,128)S(1)}, u32[]{:S(2)}, u32[]{:S(2)}) collective-permute-start(f32[1,64,128]{2,1,0:T(8,128)S(1)} %get-tuple-element.224), channel_id=1, source_target_pairs={{16,0},{17,1},{18,2},{19,3},{20,4},{21,5},{22,6},{23,7},{24,8},{25... | collective-permute-start | bytes 98312 | tf_op jit(solution)/shard_map/ppermute | solution.py:22
  142.9 9.6 %collective-permute-start.14 = (f32[34,1,128]{2,1,0:T(1,128)S(1)}, f32[34,1,128]{2,1,0:T(1,128)S(1)}, u32[]{:S(2)}, u32[]{:S(2)}) collective-permute-start(f32[34,1,128]{2,1,0:T(1,128)S(1)} %get-tuple-element.215), channel_id=1, source_target_pairs={{0,4},{4,8},{8,12},{1,5},{5,9},{9,13},{2,6},{6,10},{10,14},{3,7},{... | collective-permute-start | bytes 52232 | tf_op jit(solution)/shard_map/ppermute | solution.py:20
  150.5 5.1 %collective-permute-start.13 = (f32[34,1,128]{2,1,0:T(1,128)S(1)}, f32[34,1,128]{2,1,0:T(1,128)S(1)}, u32[]{:S(2)}, u32[]{:S(2)}) collective-permute-start(f32[34,1,128]{2,1,0:T(1,128)S(1)} %get-tuple-element.214), channel_id=1, source_target_pairs={{4,0},{8,4},{12,8},{5,1},{9,5},{13,9},{6,2},{10,6},{14,10},{7,3},{... | collective-permute-start | bytes 52232 | tf_op jit(solution)/shard_map/ppermute | solution.py:22
  157.6 9.3 %copy-start.107 = (f32[1,64,128]{2,1,0:T(8,128)S(1)}, f32[1,64,128]{2,1,0:T(8,128)}, u32[]{:S(2)}) copy-start(f32[1,64,128]{2,1,0:T(8,128)} %copy-done.106) | copy-start | bytes 98308
  161.3 13.6 %collective-permute-start.16 = (f32[34,66,1]{1,0,2:T(8,128)S(1)}, f32[34,66,1]{1,0,2:T(8,128)S(1)}, u32[]{:S(2)}, u32[]{:S(2)}) collective-permute-start(f32[34,66,1]{1,0,2:T(8,128)S(1)} %copy.399), channel_id=1, source_target_pairs={{0,1},{1,2},{2,3},{4,5},{5,6},{6,7},{8,9},{9,10},{10,11},{12,13},{... | collective-permute-start | bytes 26936 | tf_op jit(solution)/shard_map/ppermute | solution.py:20
  162.6 10.6 %collective-permute-start.15 = (f32[34,66,1]{1,0,2:T(8,128)S(1)}, f32[34,66,1]{1,0,2:T(8,128)S(1)}, u32[]{:S(2)}, u32[]{:S(2)}) collective-permute-start(f32[34,66,1]{1,0,2:T(8,128)S(1)} %copy.397), channel_id=1, source_target_pairs={{1,0},{2,1},{3,2},{5,4},{6,5},{7,6},{9,8},{10,9},{11,10},{13,12},{... | collective-permute-start | bytes 26936 | tf_op jit(solution)/shard_map/ppermute | solution.py:22
  (97 other events, 292.1 us)
where the time goes:
time: 188 us; the launch traced here: 186 us
  local copies, waits for them, and re-layouts  52.4 us (28%)
  starting transfers between devices  51.9 us (28%)
  other arithmetic  50.2 us (27%)
  blocking collectives  19.4 us (10%)
  waiting for transfers between devices  8.24 us (4%)
  between operations  3.42 us (2%)
    ppermute x7, starting transfers between devices, with_halo(): lax.ppermute(head, axis, [((i + 1) % count, i) for i in range(ends)])  26.7 us
    ppermute x7, starting transfers between devices, with_halo(): lax.ppermute(tail, axis, [(i, (i + 1) % count) for i in range(ends)])  18.4 us
    unnamed x272, local copies, waits for them, and re-layouts  15 us
    concatenate x5, other arithmetic, with_halo(): jnp.concatenate([lax.ppermute(tail, axis, [(i, (i + 1) % count) for i in...  12.2 us
    slice x7, local copies, waits for them, and re-layouts, with_halo(): head = lax.slice_in_dim(cells, 0, width, axis=dim)  11.4 us
    add x2, other arithmetic, areal_side(): return line + cy * padded[:, 1:-1, 2:] + cy_w * padded[:, 1:-1, :-2]  8.42 us
    all_gather x2, blocking collectives, body(): sides = lax.all_gather(side_pair, 'gz', axis=0, tiled=True)  8.1 us
    sub x1, other arithmetic, body(): return (field, source - applied)  7.43 us
  transfers between devices with their start and end apart: 17, of which 4 were waited for; matrix products, arithmetic and copies ran while one was open for 23% of the time, Pallas kernels for 0%

commit v1 on v0

--- a/solution.py
+++ b/solution.py
@@ -1,12 +1,15 @@
+import functools
+
 import jax
 import jax.numpy as jnp
 from jax import lax
+from jax.experimental import pallas as pl
+from jax.experimental.pallas import tpu as pltpu
 from jax.sharding import PartitionSpec as P
 
 SWEEPS = 2
-
-
 OMEGA = 0.8
+SUB, LANES = 8, 128
 
 
 def with_halo(cells, sides, width):
@@ -54,7 +57,7 @@
     return line + cy * padded[:, 1:-1, 2:] + cy_w * padded[:, 1:-1, :-2]
 
 
-def body(source, pressure, storage, trans_z, trans_x, trans_y):
+def many_blocks(source, pressure, storage, trans_z, trans_x, trans_y):
     cz = trans_z * edge_mask(trans_z, 0, lax.axis_size("gz"), lax.axis_index("gz"))
     cx = trans_x * edge_mask(trans_x, 1, lax.axis_size("ax"), lax.axis_index("ax"))
     cy = trans_y * edge_mask(trans_y, 2, lax.axis_size("ay"), lax.axis_index("ay"))
@@ -108,18 +111,490 @@
     return (field, source - applied)
 
 
+def lane_iota():
+    return lax.broadcasted_iota(jnp.int32, (SUB, LANES), 1)
+
+
+def row_iota():
+    return lax.broadcasted_iota(jnp.int32, (SUB, LANES), 0)
+
+
+def rim_slot():
+    return ((lane_iota() + 1) & (LANES - 1)) >> 1
+
+
+def tiles_of(ref, z, groups):
+    return [ref[z, SUB * x : SUB * (x + 1), :] for x in range(groups)]
+
+
+def put_tiles(ref, z, tiles):
+    for x, tile in enumerate(tiles):
+        ref[z, SUB * x : SUB * (x + 1), :] = tile
+
+
+def pack_layer(tiles, slot):
+    out = tiles[0]
+    for x, tile in enumerate(tiles[1:], 1):
+        out = jnp.where(slot == x, pltpu.roll(tile, 2 * x, 1), out)
+    return out
+
+
+def unpack_layer(rim_tile, groups):
+    return [rim_tile if x == 0 else pltpu.roll(rim_tile, LANES - 2 * x, 1) for x in range(groups)]
+
+
+def join_rims(from_south, from_north, even):
+    return jnp.where(even, pltpu.roll(from_south, 1, 1), pltpu.roll(from_north, LANES - 1, 1))
+
+
+def pack_inputs_kernel(p_ref, tx_ref, ty_ref, rim_ref, east_ref, west_ref):
+    depth, width, _ = p_ref.shape
+    groups = width // SUB
+    slot = rim_slot()
+    for which, ref in enumerate((p_ref, ty_ref)):
+        out = None
+        for z in range(depth):
+            part = pack_layer(tiles_of(ref, z, groups), slot)
+            part = pltpu.roll(part, 2 * groups * z, 1) if z else part
+            out = part if out is None else jnp.where(slot >= groups * z, part, out)
+        rim_ref[which, 0] = out
+    for z in range(depth):
+        east_ref[0, z : z + 1, :] = p_ref[z, width - 1 : width, :]
+        east_ref[1, z : z + 1, :] = tx_ref[z, SUB - 1 : SUB, :]
+        west_ref[z : z + 1, :] = p_ref[z, 0:1, :]
+
+
+def interior_couplings(tx, ty):
+    rows = lax.broadcasted_iota(jnp.int32, tx.shape, 0)
+    lanes = lax.broadcasted_iota(jnp.int32, tx.shape, 1)
+    return (
+        jnp.where(rows == tx.shape[0] - 1, 0.0, tx),
+        jnp.where(lanes == tx.shape[1] - 1, 0.0, ty),
+    )
+
+
+def interior_inflow(p, cx, cy):
+    width = p.shape[0]
+    out = cx * pltpu.roll(p, width - 1, 0) + pltpu.roll(cx * p, 1, 0)
+    return out + cy * pltpu.roll(p, LANES - 1, 1) + pltpu.roll(cy * p, 1, 1)
+
+
+def prepare_kernel(source_ref, p_ref, storage_ref, tz_ref, tx_ref, ty_ref, s_ref, b_ref, cz_ref):
+    def layer(z, _):
+        cx, cy = interior_couplings(tx_ref[z], ty_ref[z])
+        s_ref[z] = storage_ref[z] + cx + pltpu.roll(cx, 1, 0) + cy + pltpu.roll(cy, 1, 1)
+        b_ref[z] = source_ref[z] + interior_inflow(p_ref[z], cx, cy)
+        cz_ref[z] = tz_ref[z]
+        return _
+
+    lax.fori_loop(0, s_ref.shape[0], layer, 0, unroll=2)
+
+
+def line_kernel(source_ref, p_ref, tx_ref, ty_ref, b_ref):
+    def layer(z, _):
+        cx, cy = interior_couplings(tx_ref[z], ty_ref[z])
+        b_ref[z] = source_ref[z] + interior_inflow(p_ref[z], cx, cy)
+        return _
+
+    lax.fori_loop(0, b_ref.shape[0], layer, 0, unroll=2)
+
+
+def split_rims(forward, backward, first_plane):
+    return (
+        jnp.where(first_plane, forward, backward),
+        jnp.where(first_plane, backward, forward),
+    )
+
+
+def rim_at(rim_ref, z, groups):
+    per = LANES // 2 // groups
+    tile = rim_ref[z // per]
+    shift = (LANES - 2 * groups * (z % per)) % LANES
+    return unpack_layer(pltpu.roll(tile, shift, 1), groups)
+
+
+def put_rim(rim_ref, z, tiles, slot):
+    groups = len(tiles)
+    per = LANES // 2 // groups
+    tile = pltpu.roll(pack_layer(tiles, slot), 2 * groups * (z % per), 1)
+    old = rim_ref[z // per]
+    rim_ref[z // per] = jnp.where(slot // groups == z % per, tile, old)
+
+
+def eliminate_kernel(
+    s_ref, b_ref, cz_ref, own_rim_ref, own_east_ref, west_ref, east_ref, forward_ref, backward_ref,
+    c_ref, inv_ref, d_ref, face_ref, rows_ref, rim_ref, add_rows, add_rim,
+):
+    depth, width, _ = s_ref.shape
+    groups = width // SUB
+    plane, ax, ay = lax.axis_index("gz"), lax.axis_index("ax"), lax.axis_index("ay")
+    first = plane == 0
+    lane, row = lane_iota(), row_iota()
+    even = (lane & 1) == 0
+    keep_west = jnp.where(ax > 0, 1.0, 0.0)
+    keep_east = jnp.where(ax < lax.axis_size("ax") - 1, 1.0, 0.0)
+    keep_south = jnp.where(ay > 0, 1.0, 0.0)
+    keep_north = jnp.where(ay < lax.axis_size("ay") - 1, 1.0, 0.0)
+    west = west_ref[1] * keep_west
+    east = own_east_ref[1] * keep_east
+    rows_ref[0] = west
+    rows_ref[1] = east
+    add_rows[0] = west * west_ref[0]
+    add_rows[1] = east * east_ref[...]
+    for t in range(rim_ref.shape[0]):
+        south_p, north_p = split_rims(forward_ref[0, t], backward_ref[0, t], first)
+        south_c, _ = split_rims(forward_ref[1, t], backward_ref[1, t], first)
+        coupling = jnp.where(
+            even, pltpu.roll(south_c, 1, 1) * keep_south, own_rim_ref[1, t] * keep_north
+        )
+        rim_ref[t] = coupling
+        add_rim[t] = coupling * join_rims(south_p, north_p, even)
+    rim_lane = (lane == 0) | (lane == LANES - 1)
+
+    def sides(z):
+        s, b = tiles_of(s_ref, z, groups), tiles_of(b_ref, z, groups)
+        for x, (more_s, more_b) in enumerate(
+            zip(rim_at(rim_ref, z, groups), rim_at(add_rim, z, groups))
+        ):
+            s[x] = s[x] + jnp.where(rim_lane, more_s, 0.0)
+            b[x] = b[x] + jnp.where(rim_lane, more_b, 0.0)
+        for x, which, at in ((0, 0, 0), (groups - 1, 1, SUB - 1)):
+            s[x] = s[x] + jnp.where(row == at, rows_ref[which, pl.ds(z, 1), :], 0.0)
+            b[x] = b[x] + jnp.where(row == at, add_rows[which, pl.ds(z, 1), :], 0.0)
+        return s, b
+
+    def step(k, carry):
+        z = jnp.where(first, k, depth - 1 - k)
+        ez = jnp.where(first, k, depth - 2 - k)
+        q_prev, g_prev, c_prev = carry
+        s, b = sides(z)
+        e = tiles_of(cz_ref, ez, groups)
+        q = [s[x] + c_prev[x] * q_prev[x] for x in range(groups)]
+        g = [b[x] + c_prev[x] * g_prev[x] for x in range(groups)]
+        inv = [1.0 / (q[x] + e[x]) for x in range(groups)]
+        c = [e[x] * inv[x] for x in range(groups)]
+        put_tiles(c_ref, z, c)
+        put_tiles(inv_ref, z, inv)
+        put_tiles(d_ref, z, [g[x] * inv[x] for x in range(groups)])
+        return q, g, c
+
+    zero = [jnp.zeros((SUB, LANES), jnp.float32) for _ in range(groups)]
+    q, g, c = lax.fori_loop(0, depth - 1, step, (zero, zero, zero))
+    s, b = sides(jnp.where(first, depth - 1, 0))
+    put_tiles(face_ref, 0, [s[x] + c[x] * q[x] for x in range(groups)])
+    put_tiles(face_ref, 1, [b[x] + c[x] * g[x] for x in range(groups)])
+    face_ref[2] = cz_ref[depth - 1]
+
+
+def back_kernel(c_ref, d_ref, p_ref, face_ref, other_ref, f_ref, coef_ref, rim_ref, ends_ref):
+    depth, width, _ = p_ref.shape
+    groups = width // SUB
+    first = lax.axis_index("gz") == 0
+    slot = rim_slot()
+    q_a, q_b = face_ref[0], other_ref[0]
+    e = jnp.where(first, face_ref[2], other_ref[2])
+    det = 1.0 / (q_a * q_b + e * (q_a + q_b))
+    coef_ref[0] = (q_b + e) * det
+    coef_ref[1] = e * det
+    coef_ref[2] = (q_a + e) * det
+    coef_ref[3] = e
+    x = coef_ref[0] * face_ref[1] + coef_ref[1] * other_ref[1]
+    finish_back(x, c_ref, d_ref, p_ref, f_ref, rim_ref, ends_ref, first, slot)
+
+
+def finish_back(x_end, c_ref, d_ref, p_ref, f_ref, rim_ref, ends_ref, first, slot):
+    depth, width, _ = p_ref.shape
+    groups = width // SUB
+
+    def emit(z, x):
+        f = []
+        for t, p in enumerate(tiles_of(p_ref, z, groups)):
+            f.append(p + OMEGA * (x[t] - p))
+        put_tiles(f_ref, z, f)
+        put_rim(rim_ref, z, f, slot)
+        ends_ref[0, pl.ds(z, 1), :] = f[0][0:1, :]
+        ends_ref[1, pl.ds(z, 1), :] = f[-1][SUB - 1 : SUB, :]
+
+    def step(i, x):
+        k = depth - 2 - i
+        z = jnp.where(first, k, depth - 1 - k)
+        c, d = tiles_of(c_ref, z, groups), tiles_of(d_ref, z, groups)
+        x = [d[t] + c[t] * x[t] for t in range(groups)]
+        emit(z, x)
+        return x
+
+    x = [x_end[SUB * t : SUB * (t + 1), :] for t in range(groups)]
+    emit(jnp.where(first, depth - 1, 0), x)
+    lax.fori_loop(0, depth - 1, step, x)
+
+
+def eliminate_again_kernel(
+    b_ref, c_ref, inv_ref, f_ref, rows_ref, rim_ref, west_ref, east_ref, forward_ref, backward_ref,
+    d_ref, face_ref, add_rows, add_rim,
+):
+    depth, width, _ = b_ref.shape
+    groups = width // SUB
+    first = lax.axis_index("gz") == 0
+    lane, row = lane_iota(), row_iota()
+    even = (lane & 1) == 0
+    add_rows[0] = rows_ref[0] * west_ref[...]
+    add_rows[1] = rows_ref[1] * east_ref[...]
+    for t in range(rim_ref.shape[0]):
+        south, north = split_rims(forward_ref[t], backward_ref[t], first)
+        add_rim[t] = rim_ref[t] * join_rims(south, north, even)
+    rim_lane = (lane == 0) | (lane == LANES - 1)
+
+    def side(z):
+        b = tiles_of(b_ref, z, groups)
+        for x, more in enumerate(rim_at(add_rim, z, groups)):
+            b[x] = b[x] + jnp.where(rim_lane, more, 0.0)
+        for x, which, at in ((0, 0, 0), (groups - 1, 1, SUB - 1)):
+            b[x] = b[x] + jnp.where(row == at, add_rows[which, pl.ds(z, 1), :], 0.0)
+        return b
+
+    def step(k, g_prev):
+        z = jnp.where(first, k, depth - 1 - k)
+        b, inv, c = side(z), tiles_of(inv_ref, z, groups), tiles_of(c_ref, z, groups)
+        g = [b[x] + g_prev[x] for x in range(groups)]
+        put_tiles(d_ref, z, [g[x] * inv[x] for x in range(groups)])
+        return [c[x] * g[x] for x in range(groups)]
+
+    zero = [jnp.zeros((SUB, LANES), jnp.float32) for _ in range(groups)]
+    carried = lax.fori_loop(0, depth - 1, step, zero)
+    last = jnp.where(first, depth - 1, 0)
+    b = side(last)
+    put_tiles(face_ref, 0, [b[x] + carried[x] for x in range(groups)])
+    face_ref[1] = f_ref[last]
+
+
+def back_again_kernel(
+    c_ref, d_ref, p_ref, coef_ref, face_ref, other_ref, f_ref, rim_ref, ends_ref, flux_ref
+):
+    first = lax.axis_index("gz") == 0
+    slot = rim_slot()
+    own, other = face_ref[0], other_ref[0]
+    x = coef_ref[0] * own + coef_ref[1] * other
+    y = coef_ref[2] * other + coef_ref[1] * own
+    mine, theirs = face_ref[1], other_ref[1]
+    mine = mine + OMEGA * (x - mine)
+    theirs = theirs + OMEGA * (y - theirs)
+    flux_ref[...] = coef_ref[3] * (mine - theirs)
+    finish_back(x, c_ref, d_ref, p_ref, f_ref, rim_ref, ends_ref, first, slot)
+
+
+def residual_kernel(source_ref, storage_ref, tz_ref, tx_ref, ty_ref, f_ref, flux_ref, r_ref):
+    chunk, width, _ = r_ref.shape
+    depth = f_ref.shape[0]
+    start = pl.program_id(0) * chunk
+    first = lax.axis_index("gz") == 0
+
+    def layer(i, below):
+        z = start + i
+        p = f_ref[z]
+        cx, cy = interior_couplings(tx_ref[i], ty_ref[i])
+        above = tz_ref[z] * (p - f_ref[jnp.minimum(z + 1, depth - 1)])
+        gx = cx * (p - pltpu.roll(p, width - 1, 0))
+        gy = cy * (p - pltpu.roll(p, LANES - 1, 1))
+        r = source_ref[i] - storage_ref[i] * p - (gx - pltpu.roll(gx, 1, 0))
+        r_ref[i] = r - (gy - pltpu.roll(gy, 1, 1)) - (above - below)
+        return above
+
+    under = jnp.maximum(start - 1, 0)
+    below = tz_ref[under] * (f_ref[under] - f_ref[start])
+    lax.fori_loop(0, chunk, layer, below, unroll=2)
+    end = jnp.where(first, depth - 1, 0)
+
+    @pl.when((end >= start) & (end < start + chunk))
+    def _():
+        r_ref[end - start] = r_ref[end - start] - flux_ref[...]
+
+
+def rims_kernel(
+    r_ref, rows_ref, rim_ref, own_ref, ends_ref, west_ref, east_ref, forward_ref, backward_ref, out_ref
+):
+    depth, width, _ = r_ref.shape
+    groups = width // SUB
+    first = lax.axis_index("gz") == 0
+    lane, row = lane_iota(), row_iota()
+    even = (lane & 1) == 0
+    rim_lane = (lane == 0) | (lane == LANES - 1)
+    south, north = split_rims(forward_ref[0], backward_ref[0], first)
+    more = rim_ref[0] * (join_rims(south, north, even) - own_ref[0])
+    west = rows_ref[0] * (west_ref[...] - ends_ref[0])
+    east = rows_ref[1] * (east_ref[...] - ends_ref[1])
+    for z in range(depth):
+        tiles = tiles_of(r_ref, z, groups)
+        moved = pltpu.roll(more, (LANES - 2 * groups * z) % LANES, 1) if z else more
+        for x, part in enumerate(unpack_layer(moved, groups)):
+            tiles[x] = tiles[x] + jnp.where(rim_lane, part, 0.0)
+        tiles[0] = tiles[0] + jnp.where(row == 0, west[z : z + 1, :], 0.0)
+        tiles[-1] = tiles[-1] + jnp.where(row == SUB - 1, east[z : z + 1, :], 0.0)
+        put_tiles(out_ref, z, tiles)
+
+
+def ring(value, axis, step):
+    count = lax.axis_size(axis)
+    return lax.ppermute(value, axis, [(i, (i + step) % count) for i in range(count)])
+
+
+def snake(value, step):
+    count = lax.axis_size("ay")
+    order = list(range(count)) + [2 * count - 1 - i for i in range(count)]
+    total = len(order)
+    pairs = [(order[i], order[(i + step) % total]) for i in range(total)]
+    return lax.ppermute(value, ("gz", "ay"), pairs)
+
+
+def two_blocks(source, pressure, storage, trans_z, trans_x, trans_y):
+    depth, width, length = pressure.shape
+    groups = width // SUB
+    chunk = LANES // 2 // groups
+    steps = depth // chunk
+    f32 = jnp.float32
+
+    def shape(*dims):
+        return jax.ShapeDtypeStruct(dims, f32)
+
+    block = shape(depth, width, length)
+    face = shape(width, length)
+    rim = shape(steps, SUB, LANES)
+    ends = shape(2, depth, length)
+    whole = pl.BlockSpec(memory_space=pltpu.VMEM)
+    part = pl.BlockSpec((chunk, width, length), lambda i: (i, 0, 0))
+    part_rim = pl.BlockSpec((1, SUB, LANES), lambda i: (i, 0, 0))
+    part_ends = pl.BlockSpec((2, chunk, length), lambda i: (0, i, 0))
+    part_end = pl.BlockSpec((chunk, length), lambda i: (i, 0))
+
+    def cost(flops, nbytes):
+        return pl.CostEstimate(flops=flops, bytes_accessed=nbytes, transcendentals=0)
+
+    size = depth * width * length
+
+    rims, east, west = pl.pallas_call(
+        pack_inputs_kernel,
+        grid=(steps,),
+        in_specs=[part, pl.BlockSpec((chunk, SUB, length), lambda i: (i, groups - 1, 0)), part],
+        out_specs=[
+            pl.BlockSpec((2, 1, SUB, LANES), lambda i: (0, i, 0, 0)),
+            part_ends,
+            part_end,
+        ],
+        out_shape=[shape(2, steps, SUB, LANES), ends, shape(depth, length)],
+        cost_estimate=cost(4 * size, 8 * size),
+        name="pack_inputs",
+    )(pressure, trans_x, trans_y)
+
+    from_west = ring(east, "ax", 1)
+    from_east = ring(west, "ax", -1)
+    forward = snake(rims, 1)
+    backward = snake(rims, -1)
+
+    s, b, cz = pl.pallas_call(
+        prepare_kernel,
+        grid=(steps,),
+        in_specs=[part] * 6,
+        out_specs=[part] * 3,
+        out_shape=[block] * 3,
+        cost_estimate=cost(20 * size, 36 * size),
+        name="prepare",
+    )(source, pressure, storage, trans_z, trans_x, trans_y)
+
+    scratch = [pltpu.VMEM((2, depth, length), f32), pltpu.VMEM((steps, SUB, LANES), f32)]
+    c, inv, d, faces, rows, coupling = pl.pallas_call(
+        eliminate_kernel,
+        in_specs=[whole] * 9,
+        out_specs=[whole] * 6,
+        out_shape=[block, block, block, shape(3, width, length), ends, rim],
+        scratch_shapes=scratch,
+        cost_estimate=cost(30 * size, 24 * size),
+        name="eliminate",
+    )(s, b, cz, rims, east, from_west, from_east, forward, backward)
+
+    others = ring(faces, "gz", 1)
+    field, coefs, rims, edges = pl.pallas_call(
+        back_kernel,
+        in_specs=[whole] * 5,
+        out_specs=[whole] * 4,
+        out_shape=[block, shape(4, width, length), rim, ends],
+        cost_estimate=cost(10 * size, 16 * size),
+        name="back",
+    )(c, d, pressure, faces, others)
+
+    from_west = ring(edges[1], "ax", 1)
+    from_east = ring(edges[0], "ax", -1)
+    forward = snake(rims, 1)
+    backward = snake(rims, -1)
+
+    b = pl.pallas_call(
+        line_kernel,
+        grid=(steps,),
+        in_specs=[part] * 4,
+        out_specs=part,
+        out_shape=block,
+        cost_estimate=cost(16 * size, 20 * size),
+        name="line",
+    )(source, field, trans_x, trans_y)
+
+    d, faces = pl.pallas_call(
+        eliminate_again_kernel,
+        in_specs=[whole] * 10,
+        out_specs=[whole] * 2,
+        out_shape=[block, shape(2, width, length)],
+        scratch_shapes=scratch,
+        cost_estimate=cost(10 * size, 16 * size),
+        name="eliminate_again",
+    )(b, c, inv, field, rows, coupling, from_west, from_east, forward, backward)
+
+    others = ring(faces, "gz", 1)
+    field, rims, edges, flux = pl.pallas_call(
+        back_again_kernel,
+        in_specs=[whole] * 6,
+        out_specs=[whole] * 4,
+        out_shape=[block, rim, ends, face],
+        cost_estimate=cost(10 * size, 16 * size),
+        name="back_again",
+    )(c, d, field, coefs, faces, others)
+
+    from_west = ring(edges[1], "ax", 1)
+    from_east = ring(edges[0], "ax", -1)
+    forward = snake(rims, 1)
+    backward = snake(rims, -1)
+
+    r = pl.pallas_call(
+        residual_kernel,
+        grid=(steps,),
+        in_specs=[part, part, whole, part, part, whole, whole],
+        out_specs=part,
+        out_shape=block,
+        cost_estimate=cost(20 * size, 28 * size),
+        name="residual",
+    )(source, storage, trans_z, trans_x, trans_y, field, flux)
+
+    r = pl.pallas_call(
+        rims_kernel,
+        grid=(steps,),
+        in_specs=[
+            part, part_ends, part_rim, part_rim, part_ends, part_end, part_end, part_rim, part_rim
+        ],
+        out_specs=part,
+        out_shape=block,
+        cost_estimate=cost(4 * size, 8 * size),
+        name="rims",
+    )(r, rows, coupling, rims, edges, from_west, from_east, forward, backward)
+    return field, r
+
+
+def body(*args):
+    depth, width, length = args[0].shape
+    groups = width // SUB
+    fits = width % SUB == 0 and length == LANES and LANES // 2 % groups == 0
+    if lax.axis_size("gz") == 2 and fits and depth % (LANES // 2 // groups) == 0:
+        return two_blocks(*args)
+    return many_blocks(*args)
+
+
 def solution(mesh):
+    spec = P("gz", "ax", "ay")
     return jax.shard_map(
-        body,
-        mesh=mesh,
-        in_specs=(
-            P("gz", "ax", "ay"),
-            P("gz", "ax", "ay"),
-            P("gz", "ax", "ay"),
-            P("gz", "ax", "ay"),
-            P("gz", "ax", "ay"),
-            P("gz", "ax", "ay"),
-        ),
-        out_specs=(P("gz", "ax", "ay"), P("gz", "ax", "ay")),
-        check_vma=False,
+        body, mesh=mesh, in_specs=(spec,) * 6, out_specs=(spec, spec), check_vma=False
     )

time: 188 us -> 82.4 us (0.44)
  Pallas kernels: 0 us -> 56.1 us
  other arithmetic: 50.2 us -> 0 us
  local copies, waits for them, and re-layouts: 52.4 us -> 5.16 us
  starting transfers between devices: 51.9 us -> 13.7 us
  blocking collectives: 19.4 us -> 0 us
  waiting for transfers between devices: 8.24 us -> 5.2 us
  between operations: 3.42 us -> 0.81 us
    pallas_call x0 -> x9, Pallas kernels: none -> 56.1 us  [the longest x1 8.73 us: two_blocks(): pl.pallas_call(eliminate_kernel, in_specs=[whole] * 9, out_specs=[whole]...]
    ppermute x17 -> x14, starting transfers between devices: 51.9 us -> 13.7 us  [the longest x8 9.3 us: ring(): lax.ppermute(value, axis, [(i, (i + step) % count) for i in range(count)])]
    slice x25 -> x0, local copies, waits for them, and re-layouts: 21.5 us -> none  [the longest x7 11.4 us: with_halo(): head = lax.slice_in_dim(cells, 0, width, axis=dim)]
    all_gather x5 -> x0, blocking collectives: 19.4 us -> none  [the longest x2 8.1 us: body(): sides = lax.all_gather(side_pair, 'gz', axis=0, tiled=True)]
    ppermute x7 -> x0, local copies, waits for them, and re-layouts: 12.3 us -> none  [the longest x3 5.49 us: with_halo(): lax.ppermute(tail, axis, [(i, (i + 1) % count) for i in range(ends)])]
    concatenate x6 -> x0, other arithmetic: 12.3 us -> none  [the longest x5 12.2 us: with_halo(): jnp.concatenate([lax.ppermute(tail, axis, [(i, (i + 1) % count) for i in...]
    unnamed x272 -> x30, local copies, waits for them, and re-layouts: 15 us -> 3.67 us
    add x5 -> x0, other arithmetic: 10.5 us -> none  [the longest x2 8.42 us: areal_side(): return line + cy * padded[:, 1:-1, 2:] + cy_w * padded[:, 1:-1, :-2]]
  transfers between devices with their start and end apart: 17 -> 14, of which waited for: 4 -> 2; matrix products, arithmetic and copies ran while one was open for 23% -> 1% of each run, Pallas kernels for 0% -> 20%
where the time goes in v1:
time: 82.4 us; the launch traced here: 81 us
  Pallas kernels  56.1 us (68%)
  starting transfers between devices  13.7 us (17%)
  waiting for transfers between devices  5.2 us (6%)
  local copies, waits for them, and re-layouts  5.16 us (6%)
    ppermute x8, starting transfers between devices, ring(): lax.ppermute(value, axis, [(i, (i + step) % count) for i in range(count)])  9.3 us
    pallas_call x1, Pallas kernels, two_blocks(): pl.pallas_call(eliminate_kernel, in_specs=[whole] * 9, out_specs=[whole]...  8.73 us
    pallas_call x1, Pallas kernels, two_blocks(): pl.pallas_call(eliminate_again_kernel, in_specs=[whole] * 10, out_specs=[...  8.07 us
    pallas_call x1, Pallas kernels, two_blocks(): pl.pallas_call(back_kernel, in_specs=[whole] * 5, out_specs=[whole] * 4,...  7.53 us
    pallas_call x1, Pallas kernels, two_blocks(): pl.pallas_call(back_again_kernel, in_specs=[whole] * 6, out_specs=[whole]...  7.5 us
    pallas_call x1, Pallas kernels, two_blocks(): pl.pallas_call(residual_kernel, grid=(steps,), in_specs=[part, part, whol...  6.04 us
    pallas_call x1, Pallas kernels, two_blocks(): pl.pallas_call(prepare_kernel, grid=(steps,), in_specs=[part] * 6, out_sp...  5.7 us
    ppermute x8, waiting for transfers between devices, ring(): lax.ppermute(value, axis, [(i, (i + step) % count) for i in range(count)])  5.19 us
  transfers between devices with their start and end apart: 14, of which 2 were waited for; matrix products, arithmetic and copies ran while one was open for 1% of the time, Pallas kernels for 20%

profile of v1, /device:TPU:25, one launch (start us, length us, event | category | flops | bytes accessed | tf_op | source)
XLA Modules:
  0.0 81.0 jit_solution(12525587693800287978)
XLA Ops:
  0.6 3.9 %pack_inputs.1 = (f32[2,4,8,128]{3,2,1,0:T(8,128)}, f32[2,32,128]{2,1,0:T(8,128)}, f32[32,128]{1,0:T(8,128)}) custom-call(f32[32,64,128]{2,1,0:T(8,128)} %p_ref.5, f32[32,64,128]{2,1,0:T(8,128)} %tx_ref.7, f32[32,64,128]{2,1,0:T(8,128)} %ty_ref.7), custom_call_target="tpu_custom_call" | custom-call | flops 1048576 | bytes 2097152 | tf_op jit(solution)/shard_map/pack_inputs/pallas_call | solution.py:473
  4.6 1.8 %collective-permute-start = (f32[2,32,128]{2,1,0:T(8,128)}, f32[2,32,128]{2,1,0:T(8,128)S(1)}, u32[]{:S(2)}, u32[]{:S(2)}) collective-permute-start(f32[2,32,128]{2,1,0:T(8,128)} %get-tuple-element.28.own_east_ref), channel_id=1, source_target_pairs={{0,4},{4,8},{8,12},{12,0},{1,5},{5,9},{9,13},{13,1},{2,6},{6,10},{... | collective-permute-start | bytes 98312 | tf_op jit(solution)/shard_map/ppermute | solution.py:437
  6.4 0.2 collective-permute-start.3
  6.5 1.3 %collective-permute-start.2 = (f32[2,4,8,128]{3,2,1,0:T(8,128)}, f32[2,4,8,128]{3,2,1,0:T(8,128)S(1)}, u32[]{:S(2)}, u32[]{:S(2)}) collective-permute-start(f32[2,4,8,128]{3,2,1,0:T(8,128)} %get-tuple-element.27.own_rim_ref), channel_id=1, source_target_pairs={{0,1},{1,2},{2,3},{3,19},{19,18},{18,17},{17,16},{16,0},{4,5},{5,6... | collective-permute-start | bytes 98312 | tf_op jit(solution)/shard_map/ppermute | solution.py:445
  7.8 5.7 %prepare.1 = (f32[32,64,128]{2,1,0:T(8,128)}, f32[32,64,128]{2,1,0:T(8,128)}, f32[32,64,128]{2,1,0:T(8,128)}) custom-call(f32[32,64,128]{2,1,0:T(8,128)} %source_ref.5, f32[32,64,128]{2,1,0:T(8,128)} %p_ref.5, f32[32,64,128]{2,1,0:T(8,128)} %storage_ref.3, f32[32,64,128]{2,1,0:T(8,128)} %tz_ref.3, f32[32,64,128]{2,1,0:T(8,128)} %tx_ref.7, f32[32,64,128]{2,1,0:T(8,128)} %ty_ref.7), custom_call_target="tpu_custom_call" | custom-call | flops 5242880 | bytes 9437184 | tf_op jit(solution)/shard_map/prepare/pallas_call | solution.py:492
  13.6 0.5 copy-done.8
  14.2 8.7 %eliminate.1 = (f32[32,64,128]{2,1,0:T(8,128)}, f32[32,64,128]{2,1,0:T(8,128)}, f32[32,64,128]{2,1,0:T(8,128)}, f32[3,64,128]{2,1,0:T(8,128)}, f32[2,32,128]{2,1,0:T(8,128)}, /*index=5*/f32[4,8,128]{2,1,0:T(8,128)}) custom-call(f32[32,64,128]{2,1,0:T(8,128)} %get-tuple-element.24.s_ref, f32[32,64,128]{2,1,0:T(8,128)} %get-tuple-element.25.b_ref, ...), custom_call_target="tpu_custom_call" | custom-call | flops 7864320 | bytes 6291456 | tf_op jit(solution)/shard_map/eliminate/pallas_call | solution.py:503
  23.0 1.2 %collective-permute-start.4 = (f32[3,64,128]{2,1,0:T(8,128)}, f32[3,64,128]{2,1,0:T(8,128)S(1)}, u32[]{:S(2)}, u32[]{:S(2)}) collective-permute-start(f32[3,64,128]{2,1,0:T(8,128)} %get-tuple-element.32.face_ref), channel_id=1, source_target_pairs={{0,16},{16,0},{1,17},{17,1},{2,18},{18,2},{3,19},{19,3},{4,20},{20... | collective-permute-start | bytes 294920 | tf_op jit(solution)/shard_map/ppermute | solution.py:437
  24.2 2.5 %collective-permute-done.4.other_ref = f32[3,64,128]{2,1,0:T(8,128)S(1)} collective-permute-done((f32[3,64,128]{2,1,0:T(8,128)}, f32[3,64,128]{2,1,0:T(8,128)S(1)}, u32[]{:S(2)}, u32[]{:S(2)}) %collective-permute-start.4) | collective-permute-done | bytes 98336 | tf_op jit(solution)/shard_map/ppermute | solution.py:437
  26.6 0.6 copy-done
  27.3 7.5 %back.1 = (f32[32,64,128]{2,1,0:T(8,128)}, f32[4,64,128]{2,1,0:T(8,128)}, f32[4,8,128]{2,1,0:T(8,128)}, f32[2,32,128]{2,1,0:T(8,128)}) custom-call(f32[32,64,128]{2,1,0:T(8,128)} %get-tuple-element.30.c_ref, f32[32,64,128]{2,1,0:T(8,128)} %get-tuple-element.31.d_ref, f32[32,64,128]{2,1,0:T(8,128)} %p_ref.5, f32[3,64,128]{2,1,0:T(8,128)} %get-tuple-element.32.face_ref, ...), custom_call_target="tpu_custom_call" | custom-call | flops 2621440 | bytes 4194304 | tf_op jit(solution)/shard_map/back/pallas_call | solution.py:514
  34.8 0.8 slice_bitcast_fusion.2
  35.6 1.8 %collective-permute-start.6 = (f32[32,128]{1,0:T(8,128)S(1)}, f32[32,128]{1,0:T(8,128)S(1)}, u32[]{:S(2)}, u32[]{:S(2)}) collective-permute-start(f32[32,128]{1,0:T(8,128)S(1)} %get-tuple-element.48), channel_id=1, source_target_pairs={{0,12},{4,0},{8,4},{12,8},{1,13},{5,1},{9,5},{13,9},{2,14},{6,2},{... | collective-permute-start | bytes 49160 | tf_op jit(solution)/shard_map/ppermute | solution.py:437
  37.3 1.1 %collective-permute-start.5 = (f32[32,128]{1,0:T(8,128)S(1)}, f32[32,128]{1,0:T(8,128)S(1)}, u32[]{:S(2)}, u32[]{:S(2)}) collective-permute-start(f32[32,128]{1,0:T(8,128)S(1)} %get-tuple-element.49), channel_id=1, source_target_pairs={{0,4},{4,8},{8,12},{12,0},{1,5},{5,9},{9,13},{13,1},{2,6},{6,10},{... | collective-permute-start | bytes 49160 | tf_op jit(solution)/shard_map/ppermute | solution.py:437
  38.5 0.2 collective-permute-start.8
  38.6 1.3 %collective-permute-start.7 = (f32[4,8,128]{2,1,0:T(8,128)S(1)}, f32[4,8,128]{2,1,0:T(8,128)S(1)}, u32[]{:S(2)}, u32[]{:S(2)}) collective-permute-start(f32[4,8,128]{2,1,0:T(8,128)S(1)} %copy-done.14), channel_id=1, source_target_pairs={{0,1},{1,2},{2,3},{3,19},{19,18},{18,17},{17,16},{16,0},{4,5},{5,6... | collective-permute-start | bytes 49160 | tf_op jit(solution)/shard_map/ppermute | solution.py:445
  39.9 4.7 %line.1.b_ref = f32[32,64,128]{2,1,0:T(8,128)} custom-call(f32[32,64,128]{2,1,0:T(8,128)} %source_ref.5, f32[32,64,128]{2,1,0:T(8,128)} %get-tuple-element.33.p_ref.f_ref, f32[32,64,128]{2,1,0:T(8,128)} %tx_ref.7, f32[32,64,128]{2,1,0:T(8,128)} %ty_ref.7), custom_call_target="tpu_custom_call" | custom-call | flops 4194304 | bytes 5242880 | tf_op jit(solution)/shard_map/line/pallas_call | solution.py:528
  44.7 0.5 copy-done.7
  45.3 8.1 %eliminate_again.1 = (f32[32,64,128]{2,1,0:T(8,128)}, f32[2,64,128]{2,1,0:T(8,128)}) custom-call(f32[32,64,128]{2,1,0:T(8,128)} %line.1.b_ref, f32[32,64,128]{2,1,0:T(8,128)} %get-tuple-element.30.c_ref, f32[32,64,128]{2,1,0:T(8,128)} %get-tuple-element.34.inv_ref, f32[32,64,128]{2,1,0:T(8,128)} %get-tuple-element.33.p_ref.f_ref, ...), custom_call_target="tpu_custom_call" | custom-call | flops 2621440 | bytes 4194304 | tf_op jit(solution)/shard_map/eliminate_again/pallas_call | solution.py:538
  53.4 1.2 %collective-permute-start.9 = (f32[2,64,128]{2,1,0:T(8,128)}, f32[2,64,128]{2,1,0:T(8,128)S(1)}, u32[]{:S(2)}, u32[]{:S(2)}) collective-permute-start(f32[2,64,128]{2,1,0:T(8,128)} %get-tuple-element.41.face_ref), channel_id=1, source_target_pairs={{0,16},{16,0},{1,17},{17,1},{2,18},{18,2},{3,19},{19,3},{4,20},{20... | collective-permute-start | bytes 196616 | tf_op jit(solution)/shard_map/ppermute | solution.py:437
  54.6 2.7 %collective-permute-done.9.other_ref = f32[2,64,128]{2,1,0:T(8,128)S(1)} collective-permute-done((f32[2,64,128]{2,1,0:T(8,128)}, f32[2,64,128]{2,1,0:T(8,128)S(1)}, u32[]{:S(2)}, u32[]{:S(2)}) %collective-permute-start.9) | collective-permute-done | bytes 65568 | tf_op jit(solution)/shard_map/ppermute | solution.py:437
  57.3 0.6 copy-done.1
  57.9 7.5 %back_again.1 = (f32[32,64,128]{2,1,0:T(8,128)}, f32[4,8,128]{2,1,0:T(8,128)}, f32[2,32,128]{2,1,0:T(8,128)}, f32[64,128]{1,0:T(8,128)}) custom-call(f32[32,64,128]{2,1,0:T(8,128)} %get-tuple-element.30.c_ref, f32[32,64,128]{2,1,0:T(8,128)} %get-tuple-element.39.d_ref, f32[32,64,128]{2,1,0:T(8,128)} %get-tuple-element.33.p_ref.f_ref, ...), custom_call_target="tpu_custom_call" | custom-call | flops 2621440 | bytes 4194304 | tf_op jit(solution)/shard_map/back_again/pallas_call | solution.py:549
  65.4 0.2 collective-permute-start.13
  65.6 1.3 %collective-permute-start.12 = (f32[4,8,128]{2,1,0:T(8,128)}, f32[4,8,128]{2,1,0:T(8,128)S(1)}, u32[]{:S(2)}, u32[]{:S(2)}) collective-permute-start(f32[4,8,128]{2,1,0:T(8,128)} %get-tuple-element.44.own_ref), channel_id=1, source_target_pairs={{0,1},{1,2},{2,3},{3,19},{19,18},{18,17},{17,16},{16,0},{4,5},{5,6... | collective-permute-start | bytes 49160 | tf_op jit(solution)/shard_map/ppermute | solution.py:445
  66.9 0.7 slice_bitcast_fusion
  67.6 1.4 %collective-permute-start.11 = (f32[32,128]{1,0:T(8,128)S(1)}, f32[32,128]{1,0:T(8,128)S(1)}, u32[]{:S(2)}, u32[]{:S(2)}) collective-permute-start(f32[32,128]{1,0:T(8,128)S(1)} %get-tuple-element.46), channel_id=1, source_target_pairs={{0,12},{4,0},{8,4},{12,8},{1,13},{5,1},{9,5},{13,9},{2,14},{6,2},{... | collective-permute-start | bytes 49160 | tf_op jit(solution)/shard_map/ppermute | solution.py:437
  68.9 0.8 %collective-permute-start.10 = (f32[32,128]{1,0:T(8,128)S(1)}, f32[32,128]{1,0:T(8,128)S(1)}, u32[]{:S(2)}, u32[]{:S(2)}) collective-permute-start(f32[32,128]{1,0:T(8,128)S(1)} %get-tuple-element.47), channel_id=1, source_target_pairs={{0,4},{4,8},{8,12},{12,0},{1,5},{5,9},{9,13},{13,1},{2,6},{6,10},{... | collective-permute-start | bytes 49160 | tf_op jit(solution)/shard_map/ppermute | solution.py:437
  69.8 6.0 %residual.1.r_ref = f32[32,64,128]{2,1,0:T(8,128)} custom-call(f32[32,64,128]{2,1,0:T(8,128)} %source_ref.5, f32[32,64,128]{2,1,0:T(8,128)} %storage_ref.3, f32[32,64,128]{2,1,0:T(8,128)} %tz_ref.3, f32[32,64,128]{2,1,0:T(8,128)} %tx_ref.7, f32[32,64,128]{2,1,0:T(8,128)} %ty_ref.7, f32[32,64,128]{2,1,0:T(8,128)} %get-tuple-element.22.f_ref, ...), custom_call_target="tpu_custom_call" | custom-call | flops 5242880 | bytes 7340032 | tf_op jit(solution)/shard_map/residual/pallas_call | solution.py:563
  75.9 0.5 copy-done.5
  76.5 0.6 copy-done.12
  77.1 3.9 %rims.1 = f32[32,64,128]{2,1,0:T(8,128)} custom-call(f32[32,64,128]{2,1,0:T(8,128)} %residual.1.r_ref, f32[2,32,128]{2,1,0:T(8,128)} %get-tuple-element.35.rows_ref, f32[4,8,128]{2,1,0:T(8,128)} %get-tuple-element.36.rim_ref, f32[4,8,128]{2,1,0:T(8,128)} %get-tuple-element.44.own_ref, f32[2,32,128]{2,1,0:T(8,128)} %get-tuple-element.45.ends_ref, ...), custom_call_target="tpu_custom_call" | custom-call | flops 1048576 | bytes 2097152 | tf_op jit(solution)/shard_map/rims/pallas_call | solution.py:573
  (37 shorter events, 0.2 us)
Async XLA Ops:
  4.6 9.0 %collective-permute-start = (f32[2,32,128]{2,1,0:T(8,128)}, f32[2,32,128]{2,1,0:T(8,128)S(1)}, u32[]{:S(2)}, u32[]{:S(2)}) collective-permute-start(f32[2,32,128]{2,1,0:T(8,128)} %get-tuple-element.28.own_east_ref), channel_id=1, source_target_pairs={{0,4},{4,8},{8,12},{12,0},{1,5},{5,9},{9,13},{13,1},{2,6},{6,10},{... | collective-permute-start | bytes 98312 | tf_op jit(solution)/shard_map/ppermute | solution.py:437
  6.4 7.2 %collective-permute-start.3 = (f32[2,4,8,128]{3,2,1,0:T(8,128)}, f32[2,4,8,128]{3,2,1,0:T(8,128)S(1)}, u32[]{:S(2)}, u32[]{:S(2)}) collective-permute-start(f32[2,4,8,128]{3,2,1,0:T(8,128)} %get-tuple-element.27.own_rim_ref), channel_id=1, source_target_pairs={{0,16},{1,0},{2,1},{3,2},{19,3},{18,19},{17,18},{16,17},{4,20},{5,... | collective-permute-start | bytes 98312 | tf_op jit(solution)/shard_map/ppermute | solution.py:445
  6.5 7.1 %collective-permute-start.2 = (f32[2,4,8,128]{3,2,1,0:T(8,128)}, f32[2,4,8,128]{3,2,1,0:T(8,128)S(1)}, u32[]{:S(2)}, u32[]{:S(2)}) collective-permute-start(f32[2,4,8,128]{3,2,1,0:T(8,128)} %get-tuple-element.27.own_rim_ref), channel_id=1, source_target_pairs={{0,1},{1,2},{2,3},{3,19},{19,18},{18,17},{17,16},{16,0},{4,5},{5,6... | collective-permute-start | bytes 98312 | tf_op jit(solution)/shard_map/ppermute | solution.py:445
  7.8 5.7 %collective-permute-start.1 = (f32[32,128]{1,0:T(8,128)}, f32[32,128]{1,0:T(8,128)S(1)}, u32[]{:S(2)}, u32[]{:S(2)}) collective-permute-start(f32[32,128]{1,0:T(8,128)} %get-tuple-element.29), channel_id=1, source_target_pairs={{0,12},{4,0},{8,4},{12,8},{1,13},{5,1},{9,5},{13,9},{2,14},{6,2},{... | collective-permute-start | bytes 49160 | tf_op jit(solution)/shard_map/ppermute | solution.py:437
  13.5 0.6 copy-start.8
  13.6 0.6 copy-start.2
  13.6 0.6 copy-start.3
  13.6 0.6 copy-start.4
  23.0 3.7 %collective-permute-start.4 = (f32[3,64,128]{2,1,0:T(8,128)}, f32[3,64,128]{2,1,0:T(8,128)S(1)}, u32[]{:S(2)}, u32[]{:S(2)}) collective-permute-start(f32[3,64,128]{2,1,0:T(8,128)} %get-tuple-element.32.face_ref), channel_id=1, source_target_pairs={{0,16},{16,0},{1,17},{17,1},{2,18},{18,2},{3,19},{19,3},{4,20},{20... | collective-permute-start | bytes 294920 | tf_op jit(solution)/shard_map/ppermute | solution.py:437
  26.6 0.6 copy-start
  34.8 3.6 %copy-start.14 = (f32[4,8,128]{2,1,0:T(8,128)S(1)}, f32[4,8,128]{2,1,0:T(8,128)}, u32[]{:S(2)}) copy-start(f32[4,8,128]{2,1,0:T(8,128)} %get-tuple-element.38) | copy-start | bytes 49156
  35.6 9.0 %collective-permute-start.6 = (f32[32,128]{1,0:T(8,128)S(1)}, f32[32,128]{1,0:T(8,128)S(1)}, u32[]{:S(2)}, u32[]{:S(2)}) collective-permute-start(f32[32,128]{1,0:T(8,128)S(1)} %get-tuple-element.48), channel_id=1, source_target_pairs={{0,12},{4,0},{8,4},{12,8},{1,13},{5,1},{9,5},{13,9},{2,14},{6,2},{... | collective-permute-start | bytes 49160 | tf_op jit(solution)/shard_map/ppermute | solution.py:437
  37.3 7.3 %collective-permute-start.5 = (f32[32,128]{1,0:T(8,128)S(1)}, f32[32,128]{1,0:T(8,128)S(1)}, u32[]{:S(2)}, u32[]{:S(2)}) collective-permute-start(f32[32,128]{1,0:T(8,128)S(1)} %get-tuple-element.49), channel_id=1, source_target_pairs={{0,4},{4,8},{8,12},{12,0},{1,5},{5,9},{9,13},{13,1},{2,6},{6,10},{... | collective-permute-start | bytes 49160 | tf_op jit(solution)/shard_map/ppermute | solution.py:437
  38.5 6.2 %collective-permute-start.8 = (f32[4,8,128]{2,1,0:T(8,128)S(1)}, f32[4,8,128]{2,1,0:T(8,128)S(1)}, u32[]{:S(2)}, u32[]{:S(2)}) collective-permute-start(f32[4,8,128]{2,1,0:T(8,128)S(1)} %copy-done.14), channel_id=1, source_target_pairs={{0,16},{1,0},{2,1},{3,2},{19,3},{18,19},{17,18},{16,17},{4,20},{5,... | collective-permute-start | bytes 49160 | tf_op jit(solution)/shard_map/ppermute | solution.py:445
  38.6 6.0 %collective-permute-start.7 = (f32[4,8,128]{2,1,0:T(8,128)S(1)}, f32[4,8,128]{2,1,0:T(8,128)S(1)}, u32[]{:S(2)}, u32[]{:S(2)}) collective-permute-start(f32[4,8,128]{2,1,0:T(8,128)S(1)} %copy-done.14), channel_id=1, source_target_pairs={{0,1},{1,2},{2,3},{3,19},{19,18},{18,17},{17,16},{16,0},{4,5},{5,6... | collective-permute-start | bytes 49160 | tf_op jit(solution)/shard_map/ppermute | solution.py:445
  44.6 0.6 copy-start.7
  44.6 0.6 copy-start.9
  44.7 0.6 copy-start.11
  44.7 0.6 copy-start.13
  53.4 3.9 %collective-permute-start.9 = (f32[2,64,128]{2,1,0:T(8,128)}, f32[2,64,128]{2,1,0:T(8,128)S(1)}, u32[]{:S(2)}, u32[]{:S(2)}) collective-permute-start(f32[2,64,128]{2,1,0:T(8,128)} %get-tuple-element.41.face_ref), channel_id=1, source_target_pairs={{0,16},{16,0},{1,17},{17,1},{2,18},{18,2},{3,19},{19,3},{4,20},{20... | collective-permute-start | bytes 196616 | tf_op jit(solution)/shard_map/ppermute | solution.py:437
  57.3 0.6 copy-start.1
  65.4 10.4 %collective-permute-start.13 = (f32[4,8,128]{2,1,0:T(8,128)}, f32[4,8,128]{2,1,0:T(8,128)S(1)}, u32[]{:S(2)}, u32[]{:S(2)}) collective-permute-start(f32[4,8,128]{2,1,0:T(8,128)} %get-tuple-element.44.own_ref), channel_id=1, source_target_pairs={{0,16},{1,0},{2,1},{3,2},{19,3},{18,19},{17,18},{16,17},{4,20},{5,... | collective-permute-start | bytes 49160 | tf_op jit(solution)/shard_map/ppermute | solution.py:445
  65.6 10.3 %collective-permute-start.12 = (f32[4,8,128]{2,1,0:T(8,128)}, f32[4,8,128]{2,1,0:T(8,128)S(1)}, u32[]{:S(2)}, u32[]{:S(2)}) collective-permute-start(f32[4,8,128]{2,1,0:T(8,128)} %get-tuple-element.44.own_ref), channel_id=1, source_target_pairs={{0,1},{1,2},{2,3},{3,19},{19,18},{18,17},{17,16},{16,0},{4,5},{5,6... | collective-permute-start | bytes 49160 | tf_op jit(solution)/shard_map/ppermute | solution.py:445
  67.6 8.3 %collective-permute-start.11 = (f32[32,128]{1,0:T(8,128)S(1)}, f32[32,128]{1,0:T(8,128)S(1)}, u32[]{:S(2)}, u32[]{:S(2)}) collective-permute-start(f32[32,128]{1,0:T(8,128)S(1)} %get-tuple-element.46), channel_id=1, source_target_pairs={{0,12},{4,0},{8,4},{12,8},{1,13},{5,1},{9,5},{13,9},{2,14},{6,2},{... | collective-permute-start | bytes 49160 | tf_op jit(solution)/shard_map/ppermute | solution.py:437
  68.9 6.9 %collective-permute-start.10 = (f32[32,128]{1,0:T(8,128)S(1)}, f32[32,128]{1,0:T(8,128)S(1)}, u32[]{:S(2)}, u32[]{:S(2)}) collective-permute-start(f32[32,128]{1,0:T(8,128)S(1)} %get-tuple-element.47), channel_id=1, source_target_pairs={{0,4},{4,8},{8,12},{12,0},{1,5},{5,9},{9,13},{13,1},{2,6},{6,10},{... | collective-permute-start | bytes 49160 | tf_op jit(solution)/shard_map/ppermute | solution.py:437
  75.8 0.6 copy-start.5
  75.8 0.6 copy-start.6
  75.9 0.6 copy-start.10
  76.5 0.6 copy-start.12

commit v2 on v1

--- a/solution.py
+++ b/solution.py
@@ -10,6 +10,7 @@
 SWEEPS = 2
 OMEGA = 0.8
 SUB, LANES = 8, 128
+LIMIT = 16 << 20
 
 
 def with_halo(cells, sides, width):
@@ -132,35 +133,44 @@
         ref[z, SUB * x : SUB * (x + 1), :] = tile
 
 
-def pack_layer(tiles, slot):
-    out = tiles[0]
-    for x, tile in enumerate(tiles[1:], 1):
-        out = jnp.where(slot == x, pltpu.roll(tile, 2 * x, 1), out)
-    return out
-
-
-def unpack_layer(rim_tile, groups):
-    return [rim_tile if x == 0 else pltpu.roll(rim_tile, LANES - 2 * x, 1) for x in range(groups)]
-
-
 def join_rims(from_south, from_north, even):
     return jnp.where(even, pltpu.roll(from_south, 1, 1), pltpu.roll(from_north, LANES - 1, 1))
 
 
-def pack_inputs_kernel(p_ref, tx_ref, ty_ref, rim_ref, east_ref, west_ref):
+def pack_chunk(ref, start, slot, groups):
+    out = None
+    for z in range(LANES // 2 // groups):
+        for x in range(groups):
+            m = groups * z + x
+            tile = ref[start + z, SUB * x : SUB * (x + 1), :]
+            tile = pltpu.roll(tile, 2 * m, 1) if m else tile
+            out = tile if out is None else jnp.where(slot == m, tile, out)
+    return out
+
+
+def copies(pairs, sems):
+    return [pltpu.make_async_copy(src, dst, sems.at[i]) for i, (src, dst) in enumerate(pairs)]
+
+
+def pack_inputs_kernel(p_hbm, tx_hbm, ty_hbm, rim_ref, east_ref, west_ref, p_ref, tx_ref, ty_ref, sems):
     depth, width, _ = p_ref.shape
     groups = width // SUB
     slot = rim_slot()
-    for which, ref in enumerate((p_ref, ty_ref)):
-        out = None
-        for z in range(depth):
-            part = pack_layer(tiles_of(ref, z, groups), slot)
-            part = pltpu.roll(part, 2 * groups * z, 1) if z else part
-            out = part if out is None else jnp.where(slot >= groups * z, part, out)
-        rim_ref[which, 0] = out
+    chunk = LANES // 2 // groups
+    steps = depth // chunk
+    parts = [slice(i * chunk, (i + 1) * chunk) for i in range(steps)]
+    pairs = [(h.at[at], v.at[at]) for at in parts for h, v in ((p_hbm, p_ref), (ty_hbm, ty_ref))]
+    moves = copies(pairs + [(tx_hbm, tx_ref)], sems)
+    for move in moves:
+        move.start()
+    for i in range(steps):
+        for which, ref in enumerate((p_ref, ty_ref)):
+            moves[2 * i + which].wait()
+            rim_ref[which, i] = pack_chunk(ref, i * chunk, slot, groups)
+    moves[-1].wait()
     for z in range(depth):
         east_ref[0, z : z + 1, :] = p_ref[z, width - 1 : width, :]
-        east_ref[1, z : z + 1, :] = tx_ref[z, SUB - 1 : SUB, :]
+        east_ref[1, z : z + 1, :] = tx_ref[z, width - 1 : width, :]
         west_ref[z : z + 1, :] = p_ref[z, 0:1, :]
 
 
@@ -179,15 +189,34 @@
     return out + cy * pltpu.roll(p, LANES - 1, 1) + pltpu.roll(cy * p, 1, 1)
 
 
-def prepare_kernel(source_ref, p_ref, storage_ref, tz_ref, tx_ref, ty_ref, s_ref, b_ref, cz_ref):
+def prepare_kernel(
+    source_hbm, storage_hbm, tz_hbm, p_ref, tx_ref, ty_ref,
+    s_ref, b_ref, source_ref, storage_ref, tz_ref, sems,
+):
+    depth = s_ref.shape[0]
+    steps = (sems.shape[0] - 1) // 2
+    chunk = depth // steps
+    parts = [slice(i * chunk, (i + 1) * chunk) for i in range(steps)]
+    pairs = [
+        (h.at[at], v.at[at])
+        for at in parts
+        for h, v in ((storage_hbm, storage_ref), (source_hbm, source_ref))
+    ]
+    moves = copies(pairs + [(tz_hbm, tz_ref)], sems)
+    for move in moves:
+        move.start()
+
     def layer(z, _):
         cx, cy = interior_couplings(tx_ref[z], ty_ref[z])
         s_ref[z] = storage_ref[z] + cx + pltpu.roll(cx, 1, 0) + cy + pltpu.roll(cy, 1, 1)
         b_ref[z] = source_ref[z] + interior_inflow(p_ref[z], cx, cy)
-        cz_ref[z] = tz_ref[z]
         return _
 
-    lax.fori_loop(0, s_ref.shape[0], layer, 0, unroll=2)
+    for i in range(steps):
+        moves[2 * i].wait()
+        moves[2 * i + 1].wait()
+        lax.fori_loop(i * chunk, (i + 1) * chunk, layer, 0, unroll=4)
+    moves[-1].wait()
 
 
 def line_kernel(source_ref, p_ref, tx_ref, ty_ref, b_ref):
@@ -196,7 +225,7 @@
         b_ref[z] = source_ref[z] + interior_inflow(p_ref[z], cx, cy)
         return _
 
-    lax.fori_loop(0, b_ref.shape[0], layer, 0, unroll=2)
+    lax.fori_loop(0, b_ref.shape[0], layer, 0, unroll=4)
 
 
 def split_rims(forward, backward, first_plane):
@@ -206,19 +235,20 @@
     )
 
 
-def rim_at(rim_ref, z, groups):
+def rim_part(tile, inner, x, groups):
+    return pltpu.roll(tile, (LANES - 2 * x - 2 * groups * inner) % LANES, 1)
+
+
+def chunked(depth, groups, first, body, carry):
     per = LANES // 2 // groups
-    tile = rim_ref[z // per]
-    shift = (LANES - 2 * groups * (z % per)) % LANES
-    return unpack_layer(pltpu.roll(tile, shift, 1), groups)
-
-
-def put_rim(rim_ref, z, tiles, slot):
-    groups = len(tiles)
-    per = LANES // 2 // groups
-    tile = pltpu.roll(pack_layer(tiles, slot), 2 * groups * (z % per), 1)
-    old = rim_ref[z // per]
-    rim_ref[z // per] = jnp.where(slot // groups == z % per, tile, old)
+    steps = depth // per
+
+    def step(i, carry):
+        chunk = jnp.where(first, i, steps - 1 - i)
+        inner = [jnp.where(first, j, per - 1 - j) for j in range(per)]
+        return body(chunk, [(chunk * per + at, at) for at in inner], carry)
+
+    return lax.fori_loop(0, steps, step, carry)
 
 
 def eliminate_kernel(
@@ -251,38 +281,32 @@
         add_rim[t] = coupling * join_rims(south_p, north_p, even)
     rim_lane = (lane == 0) | (lane == LANES - 1)
 
-    def sides(z):
-        s, b = tiles_of(s_ref, z, groups), tiles_of(b_ref, z, groups)
-        for x, (more_s, more_b) in enumerate(
-            zip(rim_at(rim_ref, z, groups), rim_at(add_rim, z, groups))
-        ):
-            s[x] = s[x] + jnp.where(rim_lane, more_s, 0.0)
-            b[x] = b[x] + jnp.where(rim_lane, more_b, 0.0)
-        for x, which, at in ((0, 0, 0), (groups - 1, 1, SUB - 1)):
-            s[x] = s[x] + jnp.where(row == at, rows_ref[which, pl.ds(z, 1), :], 0.0)
-            b[x] = b[x] + jnp.where(row == at, add_rows[which, pl.ds(z, 1), :], 0.0)
-        return s, b
-
-    def step(k, carry):
-        z = jnp.where(first, k, depth - 1 - k)
-        ez = jnp.where(first, k, depth - 2 - k)
-        q_prev, g_prev, c_prev = carry
-        s, b = sides(z)
-        e = tiles_of(cz_ref, ez, groups)
-        q = [s[x] + c_prev[x] * q_prev[x] for x in range(groups)]
-        g = [b[x] + c_prev[x] * g_prev[x] for x in range(groups)]
-        inv = [1.0 / (q[x] + e[x]) for x in range(groups)]
-        c = [e[x] * inv[x] for x in range(groups)]
-        put_tiles(c_ref, z, c)
-        put_tiles(inv_ref, z, inv)
-        put_tiles(d_ref, z, [g[x] * inv[x] for x in range(groups)])
+    def body(chunk, layers, carry):
+        tile_s, tile_b = rim_ref[chunk], add_rim[chunk]
+        q, g, c = carry
+        for z, inner in layers:
+            ez = jnp.maximum(jnp.where(first, z, z - 1), 0)
+            s, b = tiles_of(s_ref, z, groups), tiles_of(b_ref, z, groups)
+            for x in range(groups):
+                s[x] = s[x] + jnp.where(rim_lane, rim_part(tile_s, inner, x, groups), 0.0)
+                b[x] = b[x] + jnp.where(rim_lane, rim_part(tile_b, inner, x, groups), 0.0)
+            for x, which, at in ((0, 0, 0), (groups - 1, 1, SUB - 1)):
+                s[x] = s[x] + jnp.where(row == at, rows_ref[which, pl.ds(z, 1), :], 0.0)
+                b[x] = b[x] + jnp.where(row == at, add_rows[which, pl.ds(z, 1), :], 0.0)
+            e = tiles_of(cz_ref, ez, groups)
+            q = [s[x] + c[x] * q[x] for x in range(groups)]
+            g = [b[x] + c[x] * g[x] for x in range(groups)]
+            inv = [1.0 / (q[x] + e[x]) for x in range(groups)]
+            c = [e[x] * inv[x] for x in range(groups)]
+            put_tiles(c_ref, z, c)
+            put_tiles(inv_ref, z, inv)
+            put_tiles(d_ref, z, [g[x] * inv[x] for x in range(groups)])
         return q, g, c
 
     zero = [jnp.zeros((SUB, LANES), jnp.float32) for _ in range(groups)]
-    q, g, c = lax.fori_loop(0, depth - 1, step, (zero, zero, zero))
-    s, b = sides(jnp.where(first, depth - 1, 0))
-    put_tiles(face_ref, 0, [s[x] + c[x] * q[x] for x in range(groups)])
-    put_tiles(face_ref, 1, [b[x] + c[x] * g[x] for x in range(groups)])
+    q, g, _ = chunked(depth, groups, first, body, (zero, zero, zero))
+    put_tiles(face_ref, 0, q)
+    put_tiles(face_ref, 1, g)
     face_ref[2] = cz_ref[depth - 1]
 
 
@@ -306,26 +330,24 @@
     depth, width, _ = p_ref.shape
     groups = width // SUB
 
-    def emit(z, x):
-        f = []
-        for t, p in enumerate(tiles_of(p_ref, z, groups)):
-            f.append(p + OMEGA * (x[t] - p))
-        put_tiles(f_ref, z, f)
-        put_rim(rim_ref, z, f, slot)
-        ends_ref[0, pl.ds(z, 1), :] = f[0][0:1, :]
-        ends_ref[1, pl.ds(z, 1), :] = f[-1][SUB - 1 : SUB, :]
-
-    def step(i, x):
-        k = depth - 2 - i
-        z = jnp.where(first, k, depth - 1 - k)
-        c, d = tiles_of(c_ref, z, groups), tiles_of(d_ref, z, groups)
-        x = [d[t] + c[t] * x[t] for t in range(groups)]
-        emit(z, x)
+    def body(chunk, layers, x):
+        out = jnp.zeros((SUB, LANES), jnp.float32)
+        for z, inner in layers:
+            c, d = tiles_of(c_ref, z, groups), tiles_of(d_ref, z, groups)
+            keep = z == jnp.where(first, depth - 1, 0)
+            x = [jnp.where(keep, x[t], d[t] + c[t] * x[t]) for t in range(groups)]
+            f = [p + OMEGA * (x[t] - p) for t, p in enumerate(tiles_of(p_ref, z, groups))]
+            put_tiles(f_ref, z, f)
+            for t in range(groups):
+                m = groups * inner + t
+                out = jnp.where(slot == m, pltpu.roll(f[t], (2 * m) % LANES, 1), out)
+            ends_ref[0, pl.ds(z, 1), :] = f[0][0:1, :]
+            ends_ref[1, pl.ds(z, 1), :] = f[-1][SUB - 1 : SUB, :]
+        rim_ref[chunk] = out
         return x
 
     x = [x_end[SUB * t : SUB * (t + 1), :] for t in range(groups)]
-    emit(jnp.where(first, depth - 1, 0), x)
-    lax.fori_loop(0, depth - 1, step, x)
+    chunked(depth, groups, jnp.logical_not(first), body, x)
 
 
 def eliminate_again_kernel(
@@ -344,27 +366,24 @@
         add_rim[t] = rim_ref[t] * join_rims(south, north, even)
     rim_lane = (lane == 0) | (lane == LANES - 1)
 
-    def side(z):
-        b = tiles_of(b_ref, z, groups)
-        for x, more in enumerate(rim_at(add_rim, z, groups)):
-            b[x] = b[x] + jnp.where(rim_lane, more, 0.0)
-        for x, which, at in ((0, 0, 0), (groups - 1, 1, SUB - 1)):
-            b[x] = b[x] + jnp.where(row == at, add_rows[which, pl.ds(z, 1), :], 0.0)
-        return b
-
-    def step(k, g_prev):
-        z = jnp.where(first, k, depth - 1 - k)
-        b, inv, c = side(z), tiles_of(inv_ref, z, groups), tiles_of(c_ref, z, groups)
-        g = [b[x] + g_prev[x] for x in range(groups)]
-        put_tiles(d_ref, z, [g[x] * inv[x] for x in range(groups)])
-        return [c[x] * g[x] for x in range(groups)]
+    def body(chunk, layers, carried):
+        tile_b = add_rim[chunk]
+        g = carried
+        for z, inner in layers:
+            b, inv, c = (tiles_of(ref, z, groups) for ref in (b_ref, inv_ref, c_ref))
+            for x in range(groups):
+                b[x] = b[x] + jnp.where(rim_lane, rim_part(tile_b, inner, x, groups), 0.0)
+            for x, which, at in ((0, 0, 0), (groups - 1, 1, SUB - 1)):
+                b[x] = b[x] + jnp.where(row == at, add_rows[which, pl.ds(z, 1), :], 0.0)
+            g = [b[x] + carried[x] for x in range(groups)]
+            put_tiles(d_ref, z, [g[x] * inv[x] for x in range(groups)])
+            carried = [c[x] * g[x] for x in range(groups)]
+        put_tiles(face_ref, 0, g)
+        return carried
 
     zero = [jnp.zeros((SUB, LANES), jnp.float32) for _ in range(groups)]
-    carried = lax.fori_loop(0, depth - 1, step, zero)
-    last = jnp.where(first, depth - 1, 0)
-    b = side(last)
-    put_tiles(face_ref, 0, [b[x] + carried[x] for x in range(groups)])
-    face_ref[1] = f_ref[last]
+    chunked(depth, groups, first, body, zero)
+    face_ref[1] = f_ref[jnp.where(first, depth - 1, 0)]
 
 
 def back_again_kernel(
@@ -382,31 +401,28 @@
     finish_back(x, c_ref, d_ref, p_ref, f_ref, rim_ref, ends_ref, first, slot)
 
 
-def residual_kernel(source_ref, storage_ref, tz_ref, tx_ref, ty_ref, f_ref, flux_ref, r_ref):
-    chunk, width, _ = r_ref.shape
-    depth = f_ref.shape[0]
-    start = pl.program_id(0) * chunk
+def residual_kernel(
+    source_ref, storage_ref, tz_ref, tx_ref, ty_ref, f_ref, flux_ref, r_ref, f_hbm, sem
+):
+    depth, width, _ = r_ref.shape
+    out = pltpu.make_async_copy(f_ref, f_hbm, sem)
+    out.start()
     first = lax.axis_index("gz") == 0
 
-    def layer(i, below):
-        z = start + i
+    def layer(z, below):
         p = f_ref[z]
-        cx, cy = interior_couplings(tx_ref[i], ty_ref[i])
+        cx, cy = interior_couplings(tx_ref[z], ty_ref[z])
         above = tz_ref[z] * (p - f_ref[jnp.minimum(z + 1, depth - 1)])
         gx = cx * (p - pltpu.roll(p, width - 1, 0))
         gy = cy * (p - pltpu.roll(p, LANES - 1, 1))
-        r = source_ref[i] - storage_ref[i] * p - (gx - pltpu.roll(gx, 1, 0))
-        r_ref[i] = r - (gy - pltpu.roll(gy, 1, 1)) - (above - below)
+        r = source_ref[z] - storage_ref[z] * p - (gx - pltpu.roll(gx, 1, 0))
+        r_ref[z] = r - (gy - pltpu.roll(gy, 1, 1)) - (above - below)
         return above
 
-    under = jnp.maximum(start - 1, 0)
-    below = tz_ref[under] * (f_ref[under] - f_ref[start])
-    lax.fori_loop(0, chunk, layer, below, unroll=2)
+    lax.fori_loop(0, depth, layer, jnp.zeros_like(flux_ref[...]), unroll=4)
     end = jnp.where(first, depth - 1, 0)
-
-    @pl.when((end >= start) & (end < start + chunk))
-    def _():
-        r_ref[end - start] = r_ref[end - start] - flux_ref[...]
+    r_ref[end] = r_ref[end] - flux_ref[...]
+    out.wait()
 
 
 def rims_kernel(
@@ -424,9 +440,8 @@
     east = rows_ref[1] * (east_ref[...] - ends_ref[1])
     for z in range(depth):
         tiles = tiles_of(r_ref, z, groups)
-        moved = pltpu.roll(more, (LANES - 2 * groups * z) % LANES, 1) if z else more
-        for x, part in enumerate(unpack_layer(moved, groups)):
-            tiles[x] = tiles[x] + jnp.where(rim_lane, part, 0.0)
+        for x in range(groups):
+            tiles[x] = tiles[x] + jnp.where(rim_lane, rim_part(more, z, x, groups), 0.0)
         tiles[0] = tiles[0] + jnp.where(row == 0, west[z : z + 1, :], 0.0)
         tiles[-1] = tiles[-1] + jnp.where(row == SUB - 1, east[z : z + 1, :], 0.0)
         put_tiles(out_ref, z, tiles)
@@ -460,6 +475,7 @@
     rim = shape(steps, SUB, LANES)
     ends = shape(2, depth, length)
     whole = pl.BlockSpec(memory_space=pltpu.VMEM)
+    far = pl.BlockSpec(memory_space=pltpu.HBM)
     part = pl.BlockSpec((chunk, width, length), lambda i: (i, 0, 0))
     part_rim = pl.BlockSpec((1, SUB, LANES), lambda i: (i, 0, 0))
     part_ends = pl.BlockSpec((2, chunk, length), lambda i: (0, i, 0))
@@ -469,18 +485,16 @@
         return pl.CostEstimate(flops=flops, bytes_accessed=nbytes, transcendentals=0)
 
     size = depth * width * length
-
-    rims, east, west = pl.pallas_call(
+    params = pltpu.CompilerParams(vmem_limit_bytes=LIMIT)
+
+    rims, east, west, pressure, trans_x, trans_y = pl.pallas_call(
         pack_inputs_kernel,
-        grid=(steps,),
-        in_specs=[part, pl.BlockSpec((chunk, SUB, length), lambda i: (i, groups - 1, 0)), part],
-        out_specs=[
-            pl.BlockSpec((2, 1, SUB, LANES), lambda i: (0, i, 0, 0)),
-            part_ends,
-            part_end,
-        ],
-        out_shape=[shape(2, steps, SUB, LANES), ends, shape(depth, length)],
-        cost_estimate=cost(4 * size, 8 * size),
+        in_specs=[far] * 3,
+        out_specs=[whole] * 6,
+        out_shape=[shape(2, steps, SUB, LANES), ends, shape(depth, length), block, block, block],
+        scratch_shapes=[pltpu.SemaphoreType.DMA((2 * steps + 1,))],
+        compiler_params=params,
+        cost_estimate=cost(4 * size, 24 * size),
         name="pack_inputs",
     )(pressure, trans_x, trans_y)
 
@@ -489,15 +503,16 @@
     forward = snake(rims, 1)
     backward = snake(rims, -1)
 
-    s, b, cz = pl.pallas_call(
+    s, b, source, storage, cz = pl.pallas_call(
         prepare_kernel,
-        grid=(steps,),
-        in_specs=[part] * 6,
-        out_specs=[part] * 3,
-        out_shape=[block] * 3,
+        in_specs=[far] * 3 + [whole] * 3,
+        out_specs=[whole] * 5,
+        out_shape=[block] * 5,
+        scratch_shapes=[pltpu.SemaphoreType.DMA((2 * steps + 1,))],
+        compiler_params=params,
         cost_estimate=cost(20 * size, 36 * size),
         name="prepare",
-    )(source, pressure, storage, trans_z, trans_x, trans_y)
+    )(source, storage, trans_z, pressure, trans_x, trans_y)
 
     scratch = [pltpu.VMEM((2, depth, length), f32), pltpu.VMEM((steps, SUB, LANES), f32)]
     c, inv, d, faces, rows, coupling = pl.pallas_call(
@@ -506,6 +521,7 @@
         out_specs=[whole] * 6,
         out_shape=[block, block, block, shape(3, width, length), ends, rim],
         scratch_shapes=scratch,
+        compiler_params=params,
         cost_estimate=cost(30 * size, 24 * size),
         name="eliminate",
     )(s, b, cz, rims, east, from_west, from_east, forward, backward)
@@ -516,6 +532,7 @@
         in_specs=[whole] * 5,
         out_specs=[whole] * 4,
         out_shape=[block, shape(4, width, length), rim, ends],
+        compiler_params=params,
         cost_estimate=cost(10 * size, 16 * size),
         name="back",
     )(c, d, pressure, faces, others)
@@ -527,10 +544,10 @@
 
     b = pl.pallas_call(
         line_kernel,
-        grid=(steps,),
-        in_specs=[part] * 4,
-        out_specs=part,
+        in_specs=[whole] * 4,
+        out_specs=whole,
         out_shape=block,
+        compiler_params=params,
         cost_estimate=cost(16 * size, 20 * size),
         name="line",
     )(source, field, trans_x, trans_y)
@@ -541,6 +558,7 @@
         out_specs=[whole] * 2,
         out_shape=[block, shape(2, width, length)],
         scratch_shapes=scratch,
+        compiler_params=params,
         cost_estimate=cost(10 * size, 16 * size),
         name="eliminate_again",
     )(b, c, inv, field, rows, coupling, from_west, from_east, forward, backward)
@@ -551,6 +569,7 @@
         in_specs=[whole] * 6,
         out_specs=[whole] * 4,
         out_shape=[block, rim, ends, face],
+        compiler_params=params,
         cost_estimate=cost(10 * size, 16 * size),
         name="back_again",
     )(c, d, field, coefs, faces, others)
@@ -560,15 +579,16 @@
     forward = snake(rims, 1)
     backward = snake(rims, -1)
 
-    r = pl.pallas_call(
+    r, smoothed = pl.pallas_call(
         residual_kernel,
-        grid=(steps,),
-        in_specs=[part, part, whole, part, part, whole, whole],
-        out_specs=part,
-        out_shape=block,
+        in_specs=[whole] * 7,
+        out_specs=[whole, far],
+        out_shape=[block, block],
+        scratch_shapes=[pltpu.SemaphoreType.DMA],
+        compiler_params=params,
         cost_estimate=cost(20 * size, 28 * size),
         name="residual",
-    )(source, storage, trans_z, trans_x, trans_y, field, flux)
+    )(source, storage, cz, trans_x, trans_y, field, flux)
 
     r = pl.pallas_call(
         rims_kernel,
@@ -578,10 +598,11 @@
         ],
         out_specs=part,
         out_shape=block,
+        compiler_params=params,
         cost_estimate=cost(4 * size, 8 * size),
         name="rims",
     )(r, rows, coupling, rims, edges, from_west, from_east, forward, backward)
-    return field, r
+    return smoothed, r
 
 
 def body(*args):

time: 82.4 us -> 40.3 us (0.49)
  the two profiles are of different devices: /device:TPU:25 before, /device:TPU:0 now
where the time goes in v2:
time: 40.3 us; the launch traced here: 40.1 us
  starting transfers between devices  13 us (32%)
  Pallas kernels  12 us (30%)
  waiting for transfers between devices  10.7 us (27%)
  local copies, waits for them, and re-layouts  3.68 us (9%)
  between operations  0.75 us (2%)
    ppermute x6, starting transfers between devices, snake(): return lax.ppermute(value, ('gz', 'ay'), pairs)  6.79 us
    ppermute x8, waiting for transfers between devices, ring(): lax.ppermute(value, axis, [(i, (i + step) % count) for i in range(count)])  6.61 us
    ppermute x8, starting transfers between devices, ring(): lax.ppermute(value, axis, [(i, (i + step) % count) for i in range(count)])  6.24 us
    ppermute x6, waiting for transfers between devices, snake(): return lax.ppermute(value, ('gz', 'ay'), pairs)  4.07 us
    unnamed x12, local copies, waits for them, and re-layouts  3.68 us
    pallas_call x1, Pallas kernels, two_blocks(): pl.pallas_call(rims_kernel, grid=(steps,), in_specs=[part, part_ends, par...  2.14 us
    pallas_call x1, Pallas kernels, two_blocks(): pl.pallas_call(prepare_kernel, in_specs=[far] * 3 + [whole] * 3, out_spec...  1.68 us
    pallas_call x1, Pallas kernels, two_blocks(): pl.pallas_call(residual_kernel, in_specs=[whole] * 7, out_specs=[whole, f...  1.45 us
  transfers between devices with their start and end apart: 14, of which 6 were waited for; matrix products, arithmetic and copies ran while one was open for 0% of the time, Pallas kernels for 11%

profile of v2, /device:TPU:0, one launch (start us, length us, event | category | flops | bytes accessed | tf_op | source)
XLA Modules:
  0.0 40.1 jit_solution(234076221086397754)
XLA Ops:
  0.6 1.2 %copy-done = f32[32,64,128]{2,1,0:T(8,128)S(1)} copy-done((f32[32,64,128]{2,1,0:T(8,128)S(1)}, f32[32,64,128]{2,1,0:T(8,128)}, u32[]{:S(2)}) %copy-start) | copy-done | bytes 1048600
  1.9 1.2 %copy-done.1 = f32[32,64,128]{2,1,0:T(8,128)S(1)} copy-done((f32[32,64,128]{2,1,0:T(8,128)S(1)}, f32[32,64,128]{2,1,0:T(8,128)}, u32[]{:S(2)}) %copy-start.1) | copy-done | bytes 1048600
  3.1 1.2 %copy-done.2 = f32[32,64,128]{2,1,0:T(8,128)S(1)} copy-done((f32[32,64,128]{2,1,0:T(8,128)S(1)}, f32[32,64,128]{2,1,0:T(8,128)}, u32[]{:S(2)}) %copy-start.2) | copy-done | bytes 1048600
  4.3 1.4 %pack_inputs.1 = (f32[2,4,8,128]{3,2,1,0:T(8,128)S(1)}, f32[2,32,128]{2,1,0:T(8,128)S(1)}, f32[32,128]{1,0:T(8,128)S(1)}, f32[32,64,128]{2,1,0:T(8,128)S(1)}, f3...) custom-call(f32[32,64,128]{2,1,0:T(8,128)S(1)} %copy-done, f32[32,64,128]{2,1,0:T(8,128)S(1)} %copy-done.1, ...), custom_call_target="tpu_custom_call" | custom-call | flops 1048576 | bytes 6291456 | tf_op jit(solution)/shard_map/pack_inputs/pallas_call | solution.py:490
  5.7 0.5 %collective-permute-start = (f32[2,32,128]{2,1,0:T(8,128)S(1)}, f32[2,32,128]{2,1,0:T(8,128)S(1)}, u32[]{:S(2)}, u32[]{:S(2)}) collective-permute-start(f32[2,32,128]{2,1,0:T(8,128)S(1)} %get-tuple-element.40.own_east_ref), channel_id=1, source_target_pairs={{0,4},{4,8},{8,12},{12,0},{1,5},{5,9},{9,13},{13,1},{2,6},{6,10},{... | collective-permute-start | bytes 98312 | tf_op jit(solution)/shard_map/ppermute | solution.py:452
  6.3 2.5 %collective-permute-start.3 = (f32[2,4,8,128]{3,2,1,0:T(8,128)S(1)}, f32[2,4,8,128]{3,2,1,0:T(8,128)S(1)}, u32[]{:S(2)}, u32[]{:S(2)}) collective-permute-start(f32[2,4,8,128]{3,2,1,0:T(8,128)S(1)} %get-tuple-element.39.own_rim_ref), channel_id=1, source_target_pairs={{0,16},{1,0},{2,1},{3,2},{19,3},{18,19},{17,18},{16,17},{4,20},{5,... | collective-permute-start | bytes 98312 | tf_op jit(solution)/shard_map/ppermute | solution.py:460
  8.8 0.2 collective-permute-start.2
  9.0 1.3 %collective-permute-start.1 = (f32[32,128]{1,0:T(8,128)S(1)}, f32[32,128]{1,0:T(8,128)S(1)}, u32[]{:S(2)}, u32[]{:S(2)}) collective-permute-start(f32[32,128]{1,0:T(8,128)S(1)} %get-tuple-element.41), channel_id=1, source_target_pairs={{0,12},{4,0},{8,4},{12,8},{1,13},{5,1},{9,5},{13,9},{2,14},{6,2},{... | collective-permute-start | bytes 49160 | tf_op jit(solution)/shard_map/ppermute | solution.py:452
  10.3 1.7 %prepare.1 = (f32[32,64,128]{2,1,0:T(8,128)S(1)}, f32[32,64,128]{2,1,0:T(8,128)S(1)}, f32[32,64,128]{2,1,0:T(8,128)S(1)}, f32[32,64,128]{2,1,0:T(8,128)S(1)}, f32[32,64,128]{2,1,0:T(8,128)S(1)}) custom-call(f32[32,64,128]{2,1,0:T(8,128)S(1)} %copy-done.3, f32[32,64,128]{2,1,0:T(8,128)S(1)} %copy-done.4, f32[32,64,128]{2,1,0:T(8,128)S(1)} %copy-done.5, ...), custom_call_target="tpu_custom_call" | custom-call | flops 5242880 | bytes 9437184 | tf_op jit(solution)/shard_map/prepare/pallas_call | solution.py:506
  12.0 0.0 collective-permute-done.west_ref
  12.0 0.7 %collective-permute-done.2.forward_ref = f32[2,4,8,128]{3,2,1,0:T(8,128)S(1)} collective-permute-done((f32[2,4,8,128]{3,2,1,0:T(8,128)S(1)}, f32[2,4,8,128]{3,2,1,0:T(8,128)S(1)}, u32[]{:S(2)}, u32[]{:S(2)}) %collective-permute-start.2) | collective-permute-done | bytes 32800 | tf_op jit(solution)/shard_map/ppermute | solution.py:460
  12.8 1.3 %eliminate.1 = (f32[32,64,128]{2,1,0:T(8,128)S(1)}, f32[32,64,128]{2,1,0:T(8,128)S(1)}, f32[32,64,128]{2,1,0:T(8,128)S(1)}, f32[3,64,128]{2,1,0:T(8,128)S(1)}, f...) custom-call(f32[32,64,128]{2,1,0:T(8,128)S(1)} %get-tuple-element.37.s_ref, ...), custom_call_target="tpu_custom_call" | custom-call | flops 7864320 | bytes 6291456 | tf_op jit(solution)/shard_map/eliminate/pallas_call | solution.py:518
  14.0 1.6 %collective-permute-start.4 = (f32[3,64,128]{2,1,0:T(8,128)S(1)}, f32[3,64,128]{2,1,0:T(8,128)S(1)}, u32[]{:S(2)}, u32[]{:S(2)}) collective-permute-start(f32[3,64,128]{2,1,0:T(8,128)S(1)} %get-tuple-element.44.face_ref), channel_id=1, source_target_pairs={{0,16},{16,0},{1,17},{17,1},{2,18},{18,2},{3,19},{19,3},{4,20},{20... | collective-permute-start | bytes 294920 | tf_op jit(solution)/shard_map/ppermute | solution.py:452
  15.7 3.9 %collective-permute-done.4.other_ref = f32[3,64,128]{2,1,0:T(8,128)S(1)} collective-permute-done((f32[3,64,128]{2,1,0:T(8,128)S(1)}, f32[3,64,128]{2,1,0:T(8,128)S(1)}, u32[]{:S(2)}, u32[]{:S(2)}) %collective-permute-start.4) | collective-permute-done | bytes 98336 | tf_op jit(solution)/shard_map/ppermute | solution.py:452
  19.6 0.9 %back.1 = (f32[32,64,128]{2,1,0:T(8,128)S(1)}, f32[4,64,128]{2,1,0:T(8,128)S(1)}, f32[4,8,128]{2,1,0:T(8,128)S(1)}, f32[2,32,128]{2,1,0:T(8,128)S(1)}) custom-call(f32[32,64,128]{2,1,0:T(8,128)S(1)} %get-tuple-element.42.c_ref, f32[32,64,128]{2,1,0:T(8,128)S(1)} %get-tuple-element.43.d_ref, f32[32,64,128]{2,1,0:T(8,128)S(1)} %get-tuple-element.31.p_ref, ...), custom_call_target="tpu_custom_call" | custom-call | flops 2621440 | bytes 4194304 | tf_op jit(solution)/shard_map/back/pallas_call | solution.py:530
  20.5 0.1 collective-permute-start.6
  20.6 0.5 %collective-permute-start.5 = (f32[32,128]{1,0:T(8,128)S(1)}, f32[32,128]{1,0:T(8,128)S(1)}, u32[]{:S(2)}, u32[]{:S(2)}) collective-permute-start(f32[32,128]{1,0:T(8,128)S(1)} %get-tuple-element.63), channel_id=1, source_target_pairs={{0,4},{4,8},{8,12},{12,0},{1,5},{5,9},{9,13},{13,1},{2,6},{6,10},{... | collective-permute-start | bytes 49160 | tf_op jit(solution)/shard_map/ppermute | solution.py:452
  21.1 1.5 %collective-permute-start.8 = (f32[4,8,128]{2,1,0:T(8,128)S(1)}, f32[4,8,128]{2,1,0:T(8,128)S(1)}, u32[]{:S(2)}, u32[]{:S(2)}) collective-permute-start(f32[4,8,128]{2,1,0:T(8,128)S(1)} %get-tuple-element.50), channel_id=1, source_target_pairs={{0,16},{1,0},{2,1},{3,2},{19,3},{18,19},{17,18},{16,17},{4,20},{5,... | collective-permute-start | bytes 49160 | tf_op jit(solution)/shard_map/ppermute | solution.py:460
  22.6 0.5 %collective-permute-start.7 = (f32[4,8,128]{2,1,0:T(8,128)S(1)}, f32[4,8,128]{2,1,0:T(8,128)S(1)}, u32[]{:S(2)}, u32[]{:S(2)}) collective-permute-start(f32[4,8,128]{2,1,0:T(8,128)S(1)} %get-tuple-element.50), channel_id=1, source_target_pairs={{0,1},{1,2},{2,3},{3,19},{19,18},{18,17},{17,16},{16,0},{4,5},{5,6... | collective-permute-start | bytes 49160 | tf_op jit(solution)/shard_map/ppermute | solution.py:460
  23.1 1.2 %line.1.b_ref = f32[32,64,128]{2,1,0:T(8,128)S(1)} custom-call(f32[32,64,128]{2,1,0:T(8,128)S(1)} %get-tuple-element.34.source_ref, f32[32,64,128]{2,1,0:T(8,128)S(1)} %get-tuple-element.45.p_ref.f_ref, f32[32,64,128]{2,1,0:T(8,128)S(1)} %get-tuple-element.32.tx_ref, f32[32,64,128]{2,1,0:T(8,128)S(1)} %get-tuple-element.33.ty_ref), custom_call_target="tpu_custom_call" | custom-call | flops 4194304 | bytes 5242880 | tf_op jit(solution)/shard_map/line/pallas_call | solution.py:545
  24.3 0.5 %collective-permute-done.8.backward_ref = f32[4,8,128]{2,1,0:T(8,128)S(1)} collective-permute-done((f32[4,8,128]{2,1,0:T(8,128)S(1)}, f32[4,8,128]{2,1,0:T(8,128)S(1)}, u32[]{:S(2)}, u32[]{:S(2)}) %collective-permute-start.8) | collective-permute-done | bytes 16416 | tf_op jit(solution)/shard_map/ppermute | solution.py:460
  24.9 1.5 %collective-permute-done.7.forward_ref = f32[4,8,128]{2,1,0:T(8,128)S(1)} collective-permute-done((f32[4,8,128]{2,1,0:T(8,128)S(1)}, f32[4,8,128]{2,1,0:T(8,128)S(1)}, u32[]{:S(2)}, u32[]{:S(2)}) %collective-permute-start.7) | collective-permute-done | bytes 16416 | tf_op jit(solution)/shard_map/ppermute | solution.py:460
  26.4 1.0 %eliminate_again.1 = (f32[32,64,128]{2,1,0:T(8,128)S(1)}, f32[2,64,128]{2,1,0:T(8,128)S(1)}) custom-call(f32[32,64,128]{2,1,0:T(8,128)S(1)} %line.1.b_ref, f32[32,64,128]{2,1,0:T(8,128)S(1)} %get-tuple-element.42.c_ref, f32[32,64,128]{2,1,0:T(8,128)S(1)} %get-tuple-element.46.inv_ref, f32[32,64,128]{2,1,0:T(8,128)S(1)} %get-tuple-element.45.p_ref.f_ref, ...), custom_call_target="tpu_custom_call" | custom-call | flops 2621440 | bytes 4194304 | tf_op jit(solution)/shard_map/eliminate_again/pallas_call | solution.py:555
  27.3 1.6 %collective-permute-start.9 = (f32[2,64,128]{2,1,0:T(8,128)S(1)}, f32[2,64,128]{2,1,0:T(8,128)S(1)}, u32[]{:S(2)}, u32[]{:S(2)}) collective-permute-start(f32[2,64,128]{2,1,0:T(8,128)S(1)} %get-tuple-element.53.face_ref), channel_id=1, source_target_pairs={{0,16},{16,0},{1,17},{17,1},{2,18},{18,2},{3,19},{19,3},{4,20},{20... | collective-permute-start | bytes 196616 | tf_op jit(solution)/shard_map/ppermute | solution.py:452
  29.0 2.7 %collective-permute-done.9.other_ref = f32[2,64,128]{2,1,0:T(8,128)S(1)} collective-permute-done((f32[2,64,128]{2,1,0:T(8,128)S(1)}, f32[2,64,128]{2,1,0:T(8,128)S(1)}, u32[]{:S(2)}, u32[]{:S(2)}) %collective-permute-start.9) | collective-permute-done | bytes 65568 | tf_op jit(solution)/shard_map/ppermute | solution.py:452
  31.7 0.9 %back_again.1 = (f32[32,64,128]{2,1,0:T(8,128)S(1)}, f32[4,8,128]{2,1,0:T(8,128)S(1)}, f32[2,32,128]{2,1,0:T(8,128)S(1)}, f32[64,128]{1,0:T(8,128)S(1)}) custom-call(f32[32,64,128]{2,1,0:T(8,128)S(1)} %get-tuple-element.42.c_ref, f32[32,64,128]{2,1,0:T(8,128)S(1)} %get-tuple-element.51.d_ref, f32[32,64,128]{2,1,0:T(8,128)S(1)} %get-tuple-element.45.p_ref.f_ref, ...), custom_call_target="tpu_custom_call" | custom-call | flops 2621440 | bytes 4194304 | tf_op jit(solution)/shard_map/back_again/pallas_call | solution.py:567
  32.6 1.6 %collective-permute-start.13 = (f32[4,8,128]{2,1,0:T(8,128)S(1)}, f32[4,8,128]{2,1,0:T(8,128)S(1)}, u32[]{:S(2)}, u32[]{:S(2)}) collective-permute-start(f32[4,8,128]{2,1,0:T(8,128)S(1)} %get-tuple-element.58.own_ref), channel_id=1, source_target_pairs={{0,16},{1,0},{2,1},{3,2},{19,3},{18,19},{17,18},{16,17},{4,20},{5,... | collective-permute-start | bytes 49160 | tf_op jit(solution)/shard_map/ppermute | solution.py:460
  34.2 0.4 %collective-permute-start.12 = (f32[4,8,128]{2,1,0:T(8,128)S(1)}, f32[4,8,128]{2,1,0:T(8,128)S(1)}, u32[]{:S(2)}, u32[]{:S(2)}) collective-permute-start(f32[4,8,128]{2,1,0:T(8,128)S(1)} %get-tuple-element.58.own_ref), channel_id=1, source_target_pairs={{0,1},{1,2},{2,3},{3,19},{19,18},{18,17},{17,16},{16,0},{4,5},{5,6... | collective-permute-start | bytes 49160 | tf_op jit(solution)/shard_map/ppermute | solution.py:460
  34.7 0.5 %collective-permute-start.10 = (f32[32,128]{1,0:T(8,128)S(1)}, f32[32,128]{1,0:T(8,128)S(1)}, u32[]{:S(2)}, u32[]{:S(2)}) collective-permute-start(f32[32,128]{1,0:T(8,128)S(1)} %get-tuple-element.61), channel_id=1, source_target_pairs={{0,4},{4,8},{8,12},{12,0},{1,5},{5,9},{9,13},{13,1},{2,6},{6,10},{... | collective-permute-start | bytes 49160 | tf_op jit(solution)/shard_map/ppermute | solution.py:452
  35.2 1.4 %residual.1 = (f32[32,64,128]{2,1,0:T(8,128)S(1)}, f32[32,64,128]{2,1,0:T(8,128)}) custom-call(f32[32,64,128]{2,1,0:T(8,128)S(1)} %get-tuple-element.34.source_ref, f32[32,64,128]{2,1,0:T(8,128)S(1)} %get-tuple-element.35.storage_ref, f32[32,64,128]{2,1,0:T(8,128)S(1)} %get-tuple-element.36.cz_ref.tz_ref, f32[32,64,128]{2,1,0:T(8,128)S(1)} %get-tuple-element.32.tx_ref, ...), custom_call_target="tpu_custom_call" | custom-call | flops 5242880 | bytes 7340032 | tf_op jit(solution)/shard_map/residual/pallas_call | solution.py:582
  36.7 1.3 %collective-permute-done.12.forward_ref = f32[4,8,128]{2,1,0:T(8,128)S(1)} collective-permute-done((f32[4,8,128]{2,1,0:T(8,128)S(1)}, f32[4,8,128]{2,1,0:T(8,128)S(1)}, u32[]{:S(2)}, u32[]{:S(2)}) %collective-permute-start.12) | collective-permute-done | bytes 16416 | tf_op jit(solution)/shard_map/ppermute | solution.py:460
  38.0 2.1 %rims.1 = f32[32,64,128]{2,1,0:T(8,128)} custom-call(f32[32,64,128]{2,1,0:T(8,128)S(1)} %get-tuple-element.57.r_ref, f32[2,32,128]{2,1,0:T(8,128)S(1)} %get-tuple-element.47.rows_ref, f32[4,8,128]{2,1,0:T(8,128)S(1)} %get-tuple-element.48.rim_ref, f32[4,8,128]{2,1,0:T(8,128)S(1)} %get-tuple-element.58.own_ref, f32[2,32,128]{2,1,0:T(8,128)S(1)} %get-tuple-element.59.ends_ref, ...), custom_call_target="tpu_custom_call" | custom-call | flops 1048576 | bytes 2097152 | tf_op jit(solution)/shard_map/rims/pallas_call | solution.py:593
  (19 shorter events, 0.0 us)
Async XLA Ops:
  0.6 1.2 %copy-start = (f32[32,64,128]{2,1,0:T(8,128)S(1)}, f32[32,64,128]{2,1,0:T(8,128)}, u32[]{:S(2)}) copy-start(f32[32,64,128]{2,1,0:T(8,128)} %p_hbm.1) | copy-start | bytes 3145732
  1.9 1.2 %copy-start.1 = (f32[32,64,128]{2,1,0:T(8,128)S(1)}, f32[32,64,128]{2,1,0:T(8,128)}, u32[]{:S(2)}) copy-start(f32[32,64,128]{2,1,0:T(8,128)} %tx_hbm.1) | copy-start | bytes 3145732
  3.1 1.2 %copy-start.2 = (f32[32,64,128]{2,1,0:T(8,128)S(1)}, f32[32,64,128]{2,1,0:T(8,128)}, u32[]{:S(2)}) copy-start(f32[32,64,128]{2,1,0:T(8,128)} %ty_hbm.1) | copy-start | bytes 3145732
  4.3 6.0 %copy-start.3 = (f32[32,64,128]{2,1,0:T(8,128)S(1)}, f32[32,64,128]{2,1,0:T(8,128)}, u32[]{:S(2)}) copy-start(f32[32,64,128]{2,1,0:T(8,128)} %source_hbm.1) | copy-start | bytes 3145732
  4.3 6.0 %copy-start.4 = (f32[32,64,128]{2,1,0:T(8,128)S(1)}, f32[32,64,128]{2,1,0:T(8,128)}, u32[]{:S(2)}) copy-start(f32[32,64,128]{2,1,0:T(8,128)} %storage_hbm.1) | copy-start | bytes 3145732
  4.3 6.0 %copy-start.5 = (f32[32,64,128]{2,1,0:T(8,128)S(1)}, f32[32,64,128]{2,1,0:T(8,128)}, u32[]{:S(2)}) copy-start(f32[32,64,128]{2,1,0:T(8,128)} %tz_hbm.1) | copy-start | bytes 3145732
  5.7 6.3 %collective-permute-start = (f32[2,32,128]{2,1,0:T(8,128)S(1)}, f32[2,32,128]{2,1,0:T(8,128)S(1)}, u32[]{:S(2)}, u32[]{:S(2)}) collective-permute-start(f32[2,32,128]{2,1,0:T(8,128)S(1)} %get-tuple-element.40.own_east_ref), channel_id=1, source_target_pairs={{0,4},{4,8},{8,12},{12,0},{1,5},{5,9},{9,13},{13,1},{2,6},{6,10},{... | collective-permute-start | bytes 98312 | tf_op jit(solution)/shard_map/ppermute | solution.py:452
  6.3 5.7 %collective-permute-start.3 = (f32[2,4,8,128]{3,2,1,0:T(8,128)S(1)}, f32[2,4,8,128]{3,2,1,0:T(8,128)S(1)}, u32[]{:S(2)}, u32[]{:S(2)}) collective-permute-start(f32[2,4,8,128]{3,2,1,0:T(8,128)S(1)} %get-tuple-element.39.own_rim_ref), channel_id=1, source_target_pairs={{0,16},{1,0},{2,1},{3,2},{19,3},{18,19},{17,18},{16,17},{4,20},{5,... | collective-permute-start | bytes 98312 | tf_op jit(solution)/shard_map/ppermute | solution.py:460
  8.8 3.9 %collective-permute-start.2 = (f32[2,4,8,128]{3,2,1,0:T(8,128)S(1)}, f32[2,4,8,128]{3,2,1,0:T(8,128)S(1)}, u32[]{:S(2)}, u32[]{:S(2)}) collective-permute-start(f32[2,4,8,128]{3,2,1,0:T(8,128)S(1)} %get-tuple-element.39.own_rim_ref), channel_id=1, source_target_pairs={{0,1},{1,2},{2,3},{3,19},{19,18},{18,17},{17,16},{16,0},{4,5},{5,6... | collective-permute-start | bytes 98312 | tf_op jit(solution)/shard_map/ppermute | solution.py:460
  9.0 3.0 %collective-permute-start.1 = (f32[32,128]{1,0:T(8,128)S(1)}, f32[32,128]{1,0:T(8,128)S(1)}, u32[]{:S(2)}, u32[]{:S(2)}) collective-permute-start(f32[32,128]{1,0:T(8,128)S(1)} %get-tuple-element.41), channel_id=1, source_target_pairs={{0,12},{4,0},{8,4},{12,8},{1,13},{5,1},{9,5},{13,9},{2,14},{6,2},{... | collective-permute-start | bytes 49160 | tf_op jit(solution)/shard_map/ppermute | solution.py:452
  14.0 5.6 %collective-permute-start.4 = (f32[3,64,128]{2,1,0:T(8,128)S(1)}, f32[3,64,128]{2,1,0:T(8,128)S(1)}, u32[]{:S(2)}, u32[]{:S(2)}) collective-permute-start(f32[3,64,128]{2,1,0:T(8,128)S(1)} %get-tuple-element.44.face_ref), channel_id=1, source_target_pairs={{0,16},{16,0},{1,17},{17,1},{2,18},{18,2},{3,19},{19,3},{4,20},{20... | collective-permute-start | bytes 294920 | tf_op jit(solution)/shard_map/ppermute | solution.py:452
  20.5 3.8 %collective-permute-start.6 = (f32[32,128]{1,0:T(8,128)S(1)}, f32[32,128]{1,0:T(8,128)S(1)}, u32[]{:S(2)}, u32[]{:S(2)}) collective-permute-start(f32[32,128]{1,0:T(8,128)S(1)} %get-tuple-element.62), channel_id=1, source_target_pairs={{0,12},{4,0},{8,4},{12,8},{1,13},{5,1},{9,5},{13,9},{2,14},{6,2},{... | collective-permute-start | bytes 49160 | tf_op jit(solution)/shard_map/ppermute | solution.py:452
  20.6 3.7 %collective-permute-start.5 = (f32[32,128]{1,0:T(8,128)S(1)}, f32[32,128]{1,0:T(8,128)S(1)}, u32[]{:S(2)}, u32[]{:S(2)}) collective-permute-start(f32[32,128]{1,0:T(8,128)S(1)} %get-tuple-element.63), channel_id=1, source_target_pairs={{0,4},{4,8},{8,12},{12,0},{1,5},{5,9},{9,13},{13,1},{2,6},{6,10},{... | collective-permute-start | bytes 49160 | tf_op jit(solution)/shard_map/ppermute | solution.py:452
  21.1 3.7 %collective-permute-start.8 = (f32[4,8,128]{2,1,0:T(8,128)S(1)}, f32[4,8,128]{2,1,0:T(8,128)S(1)}, u32[]{:S(2)}, u32[]{:S(2)}) collective-permute-start(f32[4,8,128]{2,1,0:T(8,128)S(1)} %get-tuple-element.50), channel_id=1, source_target_pairs={{0,16},{1,0},{2,1},{3,2},{19,3},{18,19},{17,18},{16,17},{4,20},{5,... | collective-permute-start | bytes 49160 | tf_op jit(solution)/shard_map/ppermute | solution.py:460
  22.6 3.7 %collective-permute-start.7 = (f32[4,8,128]{2,1,0:T(8,128)S(1)}, f32[4,8,128]{2,1,0:T(8,128)S(1)}, u32[]{:S(2)}, u32[]{:S(2)}) collective-permute-start(f32[4,8,128]{2,1,0:T(8,128)S(1)} %get-tuple-element.50), channel_id=1, source_target_pairs={{0,1},{1,2},{2,3},{3,19},{19,18},{18,17},{17,16},{16,0},{4,5},{5,6... | collective-permute-start | bytes 49160 | tf_op jit(solution)/shard_map/ppermute | solution.py:460
  27.3 4.3 %collective-permute-start.9 = (f32[2,64,128]{2,1,0:T(8,128)S(1)}, f32[2,64,128]{2,1,0:T(8,128)S(1)}, u32[]{:S(2)}, u32[]{:S(2)}) collective-permute-start(f32[2,64,128]{2,1,0:T(8,128)S(1)} %get-tuple-element.53.face_ref), channel_id=1, source_target_pairs={{0,16},{16,0},{1,17},{17,1},{2,18},{18,2},{3,19},{19,3},{4,20},{20... | collective-permute-start | bytes 196616 | tf_op jit(solution)/shard_map/ppermute | solution.py:452
  32.6 4.0 %collective-permute-start.13 = (f32[4,8,128]{2,1,0:T(8,128)S(1)}, f32[4,8,128]{2,1,0:T(8,128)S(1)}, u32[]{:S(2)}, u32[]{:S(2)}) collective-permute-start(f32[4,8,128]{2,1,0:T(8,128)S(1)} %get-tuple-element.58.own_ref), channel_id=1, source_target_pairs={{0,16},{1,0},{2,1},{3,2},{19,3},{18,19},{17,18},{16,17},{4,20},{5,... | collective-permute-start | bytes 49160 | tf_op jit(solution)/shard_map/ppermute | solution.py:460
  34.2 3.7 %collective-permute-start.12 = (f32[4,8,128]{2,1,0:T(8,128)S(1)}, f32[4,8,128]{2,1,0:T(8,128)S(1)}, u32[]{:S(2)}, u32[]{:S(2)}) collective-permute-start(f32[4,8,128]{2,1,0:T(8,128)S(1)} %get-tuple-element.58.own_ref), channel_id=1, source_target_pairs={{0,1},{1,2},{2,3},{3,19},{19,18},{18,17},{17,16},{16,0},{4,5},{5,6... | collective-permute-start | bytes 49160 | tf_op jit(solution)/shard_map/ppermute | solution.py:460
  34.7 3.3 %collective-permute-start.11 = (f32[32,128]{1,0:T(8,128)S(1)}, f32[32,128]{1,0:T(8,128)S(1)}, u32[]{:S(2)}, u32[]{:S(2)}) collective-permute-start(f32[32,128]{1,0:T(8,128)S(1)} %get-tuple-element.60), channel_id=1, source_target_pairs={{0,12},{4,0},{8,4},{12,8},{1,13},{5,1},{9,5},{13,9},{2,14},{6,2},{... | collective-permute-start | bytes 49160 | tf_op jit(solution)/shard_map/ppermute | solution.py:452
  34.7 3.3 %collective-permute-start.10 = (f32[32,128]{1,0:T(8,128)S(1)}, f32[32,128]{1,0:T(8,128)S(1)}, u32[]{:S(2)}, u32[]{:S(2)}) collective-permute-start(f32[32,128]{1,0:T(8,128)S(1)} %get-tuple-element.61), channel_id=1, source_target_pairs={{0,4},{4,8},{8,12},{12,0},{1,5},{5,9},{9,13},{13,1},{2,6},{6,10},{... | collective-permute-start | bytes 49160 | tf_op jit(solution)/shard_map/ppermute | solution.py:452
